TPU v7x, 512 devices: a whole 4x4x16 slice. The times are simulated.
512 devices in a mesh: blk: 64 (over z, x), day: 8 (over y, core).
Axes of the slice: x: 4, y: 4, z: 16, core: 2. Of those that a mesh axis runs over, the one named last changes fastest.
Arguments:
- input_field: float32 [2, 24, 512, 4096], P(None, 'day', 'blk'), may hold values from -6 to 6
- active_mask: int32 [512], P('blk'), may hold values from 0 to 1, as said below
- neighbours: int32 [512, 8], P('blk'), may hold values from -1 to 511, as said below
- time_taps: float32 [4], replicated, may hold values from 0.1 to 0.5
- space_taps: float32 [2, 5], replicated, may hold values from 0.1 to 0.5
- coregion_factor: float32 [2, 2], replicated, may hold values from -2.5 to 2.5
Outputs:
- covariance_product: float32 [2, 24, 512, 4096], P(None, 'day', 'blk')
Inputs may be any that keep to these rules, and one draw needn't show every extreme that they name: `active_mask`: device i along blk holds in its 8 slots, in a drawn order, the map positions i * 8 to i * 8 + 7 of a map of 16 rows of 32 positions numbered row by row; every position of the first two map rows is active, others are active at random. Entries name the global slot (device index along blk times 8 plus local slot) of the active map block beside the block in that direction, -1 where there is none or it is inactive; all entries of an inactive slot are -1. East and west neighbours are held by the same device or one place away along blk; north and south ones by the device 4 places away; the four diagonal ones by the device 4 places away or one place nearer or farther than that, and all these cases occur.
All inputs are finite; a program needn't handle non-finite values.
Results may differ from a plain program's by a relative error of at most 0.0003.
Values sent between devices are 32-bit elements; how exact they have to be, the bound alone decides.
A program may use at most 64 MiB of HBM per device.

v0:
```python
import jax
import jax.numpy as jnp
from jax import lax
from jax.sharding import PartitionSpec as P

SIDE = 64
SPACE_HALF = 4
TIME_HALF = 3
REACH = 4


def with_halo(block, sides, width):
    for axis, dim in sides:
        count = lax.axis_size(axis)
        forward = [(i, i + 1) for i in range(count - 1)]
        backward = [(target, source) for source, target in forward]
        low = lax.ppermute(
            lax.slice_in_dim(block, block.shape[dim] - width, None, axis=dim), axis, forward
        )
        high = lax.ppermute(lax.slice_in_dim(block, 0, width, axis=dim), axis, backward)
        block = jnp.concatenate([low, block, high], axis=dim)
    return block


def shifted(x, axis, by):
    length = lax.axis_size(axis)
    pairs = [(i, i + by) for i in range(length) if 0 <= i + by < length]
    return lax.ppermute(x, axis, pairs)


def full_taps(tap_list, half_width):
    return [tap_list[abs(offset - half_width)] for offset in range(2 * half_width + 1)]


def coupling(coregion_factor):
    rows_list = []
    for first in range(2):
        rows_list.append(
            jnp.stack(
                [
                    coregion_factor[first, 0] * coregion_factor[second, 0]
                    + coregion_factor[first, 1] * coregion_factor[second, 1]
                    for second in range(2)
                ]
            )
        )
    return jnp.stack(rows_list)


def mix_outputs(weights, filtered):
    return jnp.stack(
        [
            weights[0, 0] * filtered[0] + weights[0, 1] * filtered[1],
            weights[1, 0] * filtered[0] + weights[1, 1] * filtered[1],
        ]
    )


def cut_strips(blocks, half_width):
    leading = blocks.shape[:-2]
    east_strip = blocks[..., :, blocks.shape[-1] - half_width :]
    west_strip = blocks[..., :, :half_width]
    north_strip = blocks[..., :half_width, :]
    south_strip = blocks[..., blocks.shape[-2] - half_width :, :]
    return [
        strip_piece.reshape(leading + (-1,))
        for strip_piece in (east_strip, west_strip, north_strip, south_strip)
    ]


def frame(blocks, fetch_strip, half_width, block_side):
    leading = blocks.shape[:-2]
    east_face = fetch_strip(0, 1).reshape(leading + (block_side, half_width))
    west_face = fetch_strip(1, 0).reshape(leading + (block_side, half_width))
    north_face = fetch_strip(2, 3).reshape(leading + (half_width, block_side))
    south_face = fetch_strip(3, 2).reshape(leading + (half_width, block_side))
    north_east = fetch_strip(4, 3).reshape(leading + (half_width, block_side))[..., :half_width]
    north_west = fetch_strip(5, 3).reshape(leading + (half_width, block_side))[
        ..., block_side - half_width :
    ]
    south_east = fetch_strip(6, 2).reshape(leading + (half_width, block_side))[..., :half_width]
    south_west = fetch_strip(7, 2).reshape(leading + (half_width, block_side))[
        ..., block_side - half_width :
    ]
    upper_rows = jnp.concatenate([north_west, north_face, north_east], axis=-1)
    middle = jnp.concatenate([west_face, blocks, east_face], axis=-1)
    bottom = jnp.concatenate([south_west, south_face, south_east], axis=-1)
    return jnp.concatenate([upper_rows, middle, bottom], axis=-2)


def smooth(padded, taps_across, taps_down, block_side):
    across = None
    for offset in range(len(taps_across)):
        addend = taps_across[offset] * padded[..., :, offset : offset + block_side]
        across = addend if across is None else across + addend
    downward = None
    for offset in range(len(taps_down)):
        addend = taps_down[offset] * across[..., offset : offset + block_side, :]
        downward = addend if downward is None else downward + addend
    return downward


def shards(input_field, active_mask, neighbours, time_taps, space_taps, coregion_factor):
    day_count = input_field.shape[1]
    slot_count = input_field.shape[2]
    live_mask = active_mask.astype(jnp.float32)[None, None, :, None]
    masked = input_field * live_mask
    extended = with_halo(masked, (("day", 1),), TIME_HALF)
    filtered = None
    for offset in range(-TIME_HALF, TIME_HALF + 1):
        addend = (
            time_taps[abs(offset)]
            * extended[:, TIME_HALF + offset : TIME_HALF + offset + day_count]
        )
        filtered = addend if filtered is None else filtered + addend
    mixed_field = mix_outputs(coupling(coregion_factor), filtered)
    blocks = mixed_field.reshape(mixed_field.shape[:3] + (SIDE, SIDE))
    strip_list = cut_strips(blocks, SPACE_HALF)
    own_index = lax.axis_index("blk")
    strip_cells = SPACE_HALF * SIDE
    packed = jnp.concatenate(strip_list, axis=-1)
    pieces_list = []
    for offset in range(-REACH - 1, REACH + 2):
        if offset == 0:
            pieces_list.append(packed)
        else:
            pieces_list.append(shifted(packed, "blk", -offset))
    gathered = jnp.concatenate(pieces_list, axis=2)
    first_slot = (own_index - REACH - 1) * slot_count

    def fetch_strip(direction, strip):
        target = neighbours[:, direction]
        present = (target >= 0).astype(jnp.float32)[None, None, :, None]
        row_index = jnp.clip(target - first_slot, 0, gathered.shape[2] - 1)
        portion = gathered[..., strip * strip_cells : (strip + 1) * strip_cells]
        return jnp.take(portion, row_index, axis=2) * present

    padded = frame(blocks, fetch_strip, SPACE_HALF, SIDE)
    result = smooth(
        padded, full_taps(space_taps[0], SPACE_HALF), full_taps(space_taps[1], SPACE_HALF), SIDE
    )
    return result.reshape(mixed_field.shape) * live_mask


def solution(mesh):
    in_specs = (P(None, "day", "blk", None), P("blk"), P("blk", None), P(), P(), P())
    out_specs = P(None, "day", "blk", None)
    return jax.shard_map(shards, mesh=mesh, in_specs=in_specs, out_specs=out_specs, check_vma=False)
```

profile of v0, /device:TPU:71, one launch (start us, length us, event | category | flops | bytes accessed | tf_op | source)
XLA Modules:
  0.0 149.0 jit_solution(441124160373451813)
XLA Ops:
  1.9 3.8 %collective-permute-start = (f32[2,3,8,4096]{3,2,1,0:T(8,128)S(1)}, f32[2,3,8,4096]{3,2,1,0:T(8,128)S(1)}, u32[]{:S(2)}, u32[]{:S(2)}) collective-permute-start(f32[2,3,8,4096]{3,2,1,0:T(8,128)S(1)} %broadcast_multiply_fusion.1), channel_id=1, source_target_pairs={{0,1},{1,2},{2,3},{3,4},{4,5},{5,6},{6,7},{8,9},{9,10},{10,11},{11... | collective-permute-start | bytes 2359304 | tf_op jit(solution)/shard_map/ppermute | solution.py:17
  5.7 1.9 %collective-permute-start.1 = (f32[2,3,8,4096]{3,2,1,0:T(8,128)S(1)}, f32[2,3,8,4096]{3,2,1,0:T(8,128)S(1)}, u32[]{:S(2)}, u32[]{:S(2)}) collective-permute-start(f32[2,3,8,4096]{3,2,1,0:T(8,128)S(1)} %broadcast_multiply_fusion.1), channel_id=1, source_target_pairs={{1,0},{2,1},{3,2},{4,3},{5,4},{6,5},{7,6},{9,8},{10,9},{11,10},{12... | collective-permute-start | bytes 2359304 | tf_op jit(solution)/shard_map/ppermute | solution.py:20
  21.4 1.7 %fusion.31 = (f32[1,1]{1,0:T(1,128)}, f32[1,1]{1,0:T(1,128)}, f32[1,1]{1,0:T(1,128)}, f32[1,1]{1,0:T(1,128)}, f32[1,1]{1,0:T(1,128)}, /*index=5*/f32[1,1]{1,0:T(...) fusion(f32[2,5]{1,0:T(2,128)} %param.12), kind=kLoop, calls=%fused_computation.136 | loop fusion | bytes 80 | tf_op jit(solution)/shard_map/slice | solution.py:32
  25.1 2.9 %fusion.20 = f32[2,3,8,4096]{3,2,1,0:T(8,128)S(1)} fusion(f32[2,3,8,4096]{3,2,1,0:T(8,128)S(1)} %broadcast_multiply_fusion.1, f32[2,3,8,4096]{3,2,1,0:T(8,128)S(1)} %collective-permute-done.1, f32[2,3,8,4096]{3,2,1,0:T(8,128)S(1)} %collective-permute-done, f32[]{:T(128)} %bitcast.9, f32[]{:T(128)} %bitcast.8, f32[]{:T(128)} %bitcast.7, f32[]{:T(128)} %bitcast.6), kind=kLoop, calls=%fused_computation.51 | loop fusion | flops 3342336 | bytes 3145744 | tf_op jit(solution)/shard_map/add | solution.py:115
  28.0 2.5 %multiply_add_fusion = (f32[1,3,8,4096]{3,2,1,0:T(8,128)S(1)}, f32[1,3,8,4096]{3,2,1,0:T(8,128)S(1)}) fusion(f32[2,3,8,4096]{3,2,1,0:T(8,128)S(1)} %fusion.20, f32[]{:T(128)} %bitcast.14, f32[]{:T(128)} %bitcast.13, f32[]{:T(128)} %bitcast.10, f32[]{:T(128)} %bitcast.5), kind=kLoop, calls=%fused_computation.61 | loop fusion | flops 589824 | bytes 1572880 | tf_op jit(solution)/shard_map/add | solution.py:54
  31.3 1.8 %fusion.29 = (f32[2,3,8,64,4]{4,3,2,1,0:T(8,128)}, f32[2,3,8,64,4]{4,3,2,1,0:T(8,128)S(1)}) fusion(f32[2,3,8,64,64]{4,3,2,1,0:T(8,128)S(1)} %constant_dynamic-update-slice_fusion), kind=kLoop, calls=%fused_computation.134 | loop fusion | bytes 196608 | tf_op jit(solution)/shard_map/slice | solution.py:61
  33.1 4.6 %copy.56 = f32[2,3,8,64,4]{2,4,3,1,0:T(4,128)} copy(f32[2,3,8,64,4]{4,3,2,1,0:T(8,128)} %get-tuple-element.26) | data formatting | bytes 98304 | tf_op jit(solution)/shard_map/slice | solution.py:61
  39.1 3.2 %copy.57 = f32[2,3,8,64,4]{2,4,3,1,0:T(4,128)} copy(f32[2,3,8,64,4]{4,3,2,1,0:T(8,128)S(1)} %get-tuple-element.27) | data formatting | bytes 98304 | tf_op jit(solution)/shard_map/slice | solution.py:62
  44.1 6.0 %collective-permute-start.2 = (f32[2,3,8,1024]{3,0,2,1:T(2,128)S(1)}, f32[2,3,8,1024]{3,0,2,1:T(2,128)S(1)}, u32[]{:S(2)}, u32[]{:S(2)}) collective-permute-start(f32[2,3,8,1024]{3,0,2,1:T(2,128)S(1)} %pad_maximum_fusion.3), channel_id=1, source_target_pairs={{0,40},{8,48},{16,56},{24,64},{32,72},{40,80},{48,88},{56,96},{64,... | collective-permute-start | bytes 589832 | tf_op jit(solution)/shard_map/ppermute | solution.py:28
  50.7 3.5 %collective-permute-start.3 = (f32[2,3,8,1024]{3,0,2,1:T(2,128)S(1)}, f32[2,3,8,1024]{3,0,2,1:T(2,128)S(1)}, u32[]{:S(2)}, u32[]{:S(2)}) collective-permute-start(f32[2,3,8,1024]{3,0,2,1:T(2,128)S(1)} %pad_maximum_fusion.3), channel_id=1, source_target_pairs={{0,32},{8,40},{16,48},{24,56},{32,64},{40,72},{48,80},{56,88},{64,... | collective-permute-start | bytes 589832 | tf_op jit(solution)/shard_map/ppermute | solution.py:28
  54.3 3.2 %collective-permute-start.4 = (f32[2,3,8,1024]{3,0,2,1:T(2,128)S(1)}, f32[2,3,8,1024]{3,0,2,1:T(2,128)S(1)}, u32[]{:S(2)}, u32[]{:S(2)}) collective-permute-start(f32[2,3,8,1024]{3,0,2,1:T(2,128)S(1)} %pad_maximum_fusion.3), channel_id=1, source_target_pairs={{0,24},{8,32},{16,40},{24,48},{32,56},{40,64},{48,72},{56,80},{64,... | collective-permute-start | bytes 589832 | tf_op jit(solution)/shard_map/ppermute | solution.py:28
  57.5 4.4 %collective-permute-start.5 = (f32[2,3,8,1024]{3,0,2,1:T(2,128)S(1)}, f32[2,3,8,1024]{3,0,2,1:T(2,128)S(1)}, u32[]{:S(2)}, u32[]{:S(2)}) collective-permute-start(f32[2,3,8,1024]{3,0,2,1:T(2,128)S(1)} %pad_maximum_fusion.3), channel_id=1, source_target_pairs={{0,16},{8,24},{16,32},{24,40},{32,48},{40,56},{48,64},{56,72},{64,... | collective-permute-start | bytes 589832 | tf_op jit(solution)/shard_map/ppermute | solution.py:28
  61.9 3.7 %collective-permute-start.6 = (f32[2,3,8,1024]{3,0,2,1:T(2,128)S(1)}, f32[2,3,8,1024]{3,0,2,1:T(2,128)S(1)}, u32[]{:S(2)}, u32[]{:S(2)}) collective-permute-start(f32[2,3,8,1024]{3,0,2,1:T(2,128)S(1)} %pad_maximum_fusion.3), channel_id=1, source_target_pairs={{0,8},{8,16},{16,24},{24,32},{32,40},{40,48},{48,56},{56,64},{64,7... | collective-permute-start | bytes 589832 | tf_op jit(solution)/shard_map/ppermute | solution.py:28
  65.6 1.9 %collective-permute-start.7 = (f32[2,3,8,1024]{3,0,2,1:T(2,128)S(1)}, f32[2,3,8,1024]{3,0,2,1:T(2,128)S(1)}, u32[]{:S(2)}, u32[]{:S(2)}) collective-permute-start(f32[2,3,8,1024]{3,0,2,1:T(2,128)S(1)} %pad_maximum_fusion.3), channel_id=1, source_target_pairs={{8,0},{16,8},{24,16},{32,24},{40,32},{48,40},{56,48},{64,56},{72,6... | collective-permute-start | bytes 589832 | tf_op jit(solution)/shard_map/ppermute | solution.py:28
  67.6 2.7 %collective-permute-start.8 = (f32[2,3,8,1024]{3,0,2,1:T(2,128)S(1)}, f32[2,3,8,1024]{3,0,2,1:T(2,128)S(1)}, u32[]{:S(2)}, u32[]{:S(2)}) collective-permute-start(f32[2,3,8,1024]{3,0,2,1:T(2,128)S(1)} %pad_maximum_fusion.3), channel_id=1, source_target_pairs={{16,0},{24,8},{32,16},{40,24},{48,32},{56,40},{64,48},{72,56},{80,... | collective-permute-start | bytes 589832 | tf_op jit(solution)/shard_map/ppermute | solution.py:28
  70.4 3.5 %collective-permute-start.9 = (f32[2,3,8,1024]{3,0,2,1:T(2,128)S(1)}, f32[2,3,8,1024]{3,0,2,1:T(2,128)S(1)}, u32[]{:S(2)}, u32[]{:S(2)}) collective-permute-start(f32[2,3,8,1024]{3,0,2,1:T(2,128)S(1)} %pad_maximum_fusion.3), channel_id=1, source_target_pairs={{24,0},{32,8},{40,16},{48,24},{56,32},{64,40},{72,48},{80,56},{88,... | collective-permute-start | bytes 589832 | tf_op jit(solution)/shard_map/ppermute | solution.py:28
  73.9 1.9 %collective-permute-start.10 = (f32[2,3,8,1024]{3,0,2,1:T(2,128)S(1)}, f32[2,3,8,1024]{3,0,2,1:T(2,128)S(1)}, u32[]{:S(2)}, u32[]{:S(2)}) collective-permute-start(f32[2,3,8,1024]{3,0,2,1:T(2,128)S(1)} %pad_maximum_fusion.3), channel_id=1, source_target_pairs={{32,0},{40,8},{48,16},{56,24},{64,32},{72,40},{80,48},{88,56},{96,... | collective-permute-start | bytes 589832 | tf_op jit(solution)/shard_map/ppermute | solution.py:28
  75.9 2.1 %collective-permute-start.11 = (f32[2,3,8,1024]{3,0,2,1:T(2,128)S(1)}, f32[2,3,8,1024]{3,0,2,1:T(2,128)S(1)}, u32[]{:S(2)}, u32[]{:S(2)}) collective-permute-start(f32[2,3,8,1024]{3,0,2,1:T(2,128)S(1)} %pad_maximum_fusion.3), channel_id=1, source_target_pairs={{40,0},{48,8},{56,16},{64,24},{72,32},{80,40},{88,48},{96,56},{104... | collective-permute-start | bytes 589832 | tf_op jit(solution)/shard_map/ppermute | solution.py:28
  78.4 2.1 %collective-permute-done.8 = f32[2,3,8,1024]{3,0,2,1:T(2,128)S(1)} collective-permute-done((f32[2,3,8,1024]{3,0,2,1:T(2,128)S(1)}, f32[2,3,8,1024]{3,0,2,1:T(2,128)S(1)}, u32[]{:S(2)}, u32[]{:S(2)}) %collective-permute-start.8) | collective-permute-done | bytes 196640 | tf_op jit(solution)/shard_map/ppermute | solution.py:28
  82.4 18.4 %collective-permute-done.11 = f32[2,3,8,1024]{3,0,2,1:T(2,128)S(1)} collective-permute-done((f32[2,3,8,1024]{3,0,2,1:T(2,128)S(1)}, f32[2,3,8,1024]{3,0,2,1:T(2,128)S(1)}, u32[]{:S(2)}, u32[]{:S(2)}) %collective-permute-start.11) | collective-permute-done | bytes 196640 | tf_op jit(solution)/shard_map/ppermute | solution.py:28
  100.8 1.8 %fusion.28 = (f32[2,3,88,256]{3,0,2,1:T(2,128)}, f32[2,3,88,256]{3,0,2,1:T(2,128)S(1)}, f32[2,3,88,256]{3,0,2,1:T(2,128)}, f32[2,3,88,256]{3,0,2,1:T(2,128)S(1)}) fusion(f32[2,3,88,1024]{3,0,2,1:T(2,128)S(1)} %constant_dynamic-update-slice_fusion.2), kind=kLoop, calls=%fused_computation.133 | loop fusion | bytes 4325376 | tf_op jit(solution)/shard_map/slice | solution.py:135
  107.2 3.5 %copy.69 = f32[2,3,8,64,4]{4,3,2,1,0:T(8,128)S(1)} copy(f32[2,3,8,64,4]{2,4,3,1,0:T(4,128)} %bitcast.67) | data formatting | bytes 98304 | tf_op jit(solution)/shard_map/reshape | solution.py:74
  110.7 1.7 %gather_fusion.4 = f32[8,2,3,256]{3,1,2,0:T(2,128)S(1)} fusion(f32[2,3,88,256]{3,0,2,1:T(2,128)} %get-tuple-element.24, s32[1024]{0:T(1024)S(1)} %pad_clamp_fusion.3), kind=kCustom, calls=%fused_computation.4.clone | custom fusion | bytes 98336 | tf_op jit(solution)/shard_map/jit(_take)/gather | solution.py:136
  114.2 4.6 %copy.70 = f32[2,3,8,64,4]{4,3,2,1,0:T(8,128)} copy(f32[2,3,8,64,4]{2,4,3,1,0:T(4,128)} %bitcast.68) | data formatting | bytes 98304 | tf_op jit(solution)/shard_map/reshape | solution.py:73
  118.8 1.7 %gather_fusion = f32[8,2,3,256]{3,1,2,0:T(2,128)S(1)} fusion(f32[2,3,88,256]{3,0,2,1:T(2,128)} %get-tuple-element.22, s32[1024]{0:T(1024)S(1)} %pad_clamp_fusion.7), kind=kCustom, calls=%fused_computation.clone | custom fusion | bytes 98336 | tf_op jit(solution)/shard_map/jit(_take)/gather | solution.py:136
  123.5 1.8 %gather_fusion.2 = f32[8,2,3,256]{3,1,2,0:T(2,128)S(1)} fusion(f32[2,3,88,256]{3,0,2,1:T(2,128)} %get-tuple-element.22, s32[1024]{0:T(1024)} %pad_clamp_fusion.5), kind=kCustom, calls=%fused_computation.2.clone | custom fusion | bytes 98336 | tf_op jit(solution)/shard_map/jit(_take)/gather | solution.py:136
  127.6 2.3 %gather_fusion.1 = f32[8,2,3,256]{3,1,2,0:T(2,128)} fusion(f32[2,3,88,256]{3,0,2,1:T(2,128)} %get-tuple-element.22, s32[1024]{0:T(1024)S(1)} %pad_clamp_fusion.6), kind=kCustom, calls=%fused_computation.1.clone | custom fusion | bytes 98336 | tf_op jit(solution)/shard_map/jit(_take)/gather | solution.py:136
  129.9 1.5 %bitcast_multiply_fusion.6 = f32[2,3,8,256]{3,0,1,2:T(2,128)} fusion(f32[8,2,3,256]{3,1,2,0:T(2,128)} %gather_fusion.1, pred[8]{0:T(512)(128)(4,1)} %get-tuple-element.70, f32[8]{0:T(128)S(1)} %copy-done.3), kind=kLoop, calls=%fused_computation.74 | loop fusion | flops 24576 | bytes 98344 | tf_op jit(solution)/shard_map/mul | solution.py:136
  131.4 1.6 %reshape.205 = f32[2,3,8,4,64]{4,3,0,1,2:T(4,128)} reshape(f32[2,3,8,256]{3,0,1,2:T(2,128)} %bitcast_multiply_fusion.6) | data formatting | bytes 98304 | tf_op jit(solution)/shard_map/reshape | solution.py:75
  133.2 2.5 %pad_maximum_fusion = f32[2,3,8,72,72]{4,3,2,1,0:T(8,128)S(1)} fusion(f32[2,3,8,64,4]{4,3,2,1,0:T(8,128)} %copy.70, f32[2,3,8,64,64]{4,3,2,1,0:T(8,128)S(1)} %constant_dynamic-update-slice_fusion, f32[2,3,8,64,4]{4,3,2,1,0:T(8,128)S(1)} %copy.69, f32[2,3,8,4,4]{4,3,0,1,2:T(4,128)S(1)} %bitcast.70, f32[2,3,8,4,64]{4,3,0,1,2:T(4,128)} %reshape.205, ...), kind=kLoop, calls=%fused_computation.25 | loop fusion | flops 1022976 | bytes 1990656 | tf_op jit(solution)/shard_map/concatenate | solution.py:88
  135.7 6.8 %fusion = f32[2,3,8,72,64]{4,3,2,1,0:T(8,128)S(1)} fusion(f32[2,3,8,72,72]{4,3,2,1,0:T(8,128)S(1)} %pad_maximum_fusion, f32[]{:T(128)} %bitcast.30, f32[]{:T(128)} %bitcast.29, f32[]{:T(128)} %bitcast.28, f32[]{:T(128)} %bitcast.27, f32[]{:T(128)} %bitcast.1), kind=kLoop, calls=%fused_computation.9 | loop fusion | flops 3760128 | bytes 8847380 | tf_op jit(solution)/shard_map/add | solution.py:95
  142.5 4.8 %fusion.8 = f32[2,3,8,64,64]{4,3,2,1,0:T(8,128)S(1)} fusion(f32[2,3,8,72,64]{4,3,2,1,0:T(8,128)S(1)} %fusion, f32[]{:T(128)} %bitcast.34, f32[]{:T(128)} %bitcast.33, f32[]{:T(128)} %bitcast.32, f32[]{:T(128)} %bitcast.31, f32[]{:T(128)} %bitcast), kind=kLoop, calls=%fused_computation.27 | loop fusion | flops 3342336 | bytes 7864340 | tf_op jit(solution)/shard_map/add | solution.py:99
  (95 shorter events, 30.4 us)
Async XLA Ops:
  0.0 23.1 %copy-start = (s32[8,8]{1,0:T(8,128)S(1)}, s32[8,8]{1,0:T(8,128)}, u32[]{:S(2)}) copy-start(s32[8,8]{1,0:T(8,128)} %param.10) | copy-start | bytes 772
  0.7 1.3 copy-start.1
  1.9 23.2 %collective-permute-start = (f32[2,3,8,4096]{3,2,1,0:T(8,128)S(1)}, f32[2,3,8,4096]{3,2,1,0:T(8,128)S(1)}, u32[]{:S(2)}, u32[]{:S(2)}) collective-permute-start(f32[2,3,8,4096]{3,2,1,0:T(8,128)S(1)} %broadcast_multiply_fusion.1), channel_id=1, source_target_pairs={{0,1},{1,2},{2,3},{3,4},{4,5},{5,6},{6,7},{8,9},{9,10},{10,11},{11... | collective-permute-start | bytes 2359304 | tf_op jit(solution)/shard_map/ppermute | solution.py:17
  5.7 19.4 %collective-permute-start.1 = (f32[2,3,8,4096]{3,2,1,0:T(8,128)S(1)}, f32[2,3,8,4096]{3,2,1,0:T(8,128)S(1)}, u32[]{:S(2)}, u32[]{:S(2)}) collective-permute-start(f32[2,3,8,4096]{3,2,1,0:T(8,128)S(1)} %broadcast_multiply_fusion.1), channel_id=1, source_target_pairs={{1,0},{2,1},{3,2},{4,3},{5,4},{6,5},{7,6},{9,8},{10,9},{11,10},{12... | collective-permute-start | bytes 2359304 | tf_op jit(solution)/shard_map/ppermute | solution.py:20
  44.1 21.5 %collective-permute-start.2 = (f32[2,3,8,1024]{3,0,2,1:T(2,128)S(1)}, f32[2,3,8,1024]{3,0,2,1:T(2,128)S(1)}, u32[]{:S(2)}, u32[]{:S(2)}) collective-permute-start(f32[2,3,8,1024]{3,0,2,1:T(2,128)S(1)} %pad_maximum_fusion.3), channel_id=1, source_target_pairs={{0,40},{8,48},{16,56},{24,64},{32,72},{40,80},{48,88},{56,96},{64,... | collective-permute-start | bytes 589832 | tf_op jit(solution)/shard_map/ppermute | solution.py:28
  50.7 16.8 %collective-permute-start.3 = (f32[2,3,8,1024]{3,0,2,1:T(2,128)S(1)}, f32[2,3,8,1024]{3,0,2,1:T(2,128)S(1)}, u32[]{:S(2)}, u32[]{:S(2)}) collective-permute-start(f32[2,3,8,1024]{3,0,2,1:T(2,128)S(1)} %pad_maximum_fusion.3), channel_id=1, source_target_pairs={{0,32},{8,40},{16,48},{24,56},{32,64},{40,72},{48,80},{56,88},{64,... | collective-permute-start | bytes 589832 | tf_op jit(solution)/shard_map/ppermute | solution.py:28
  54.3 16.1 %collective-permute-start.4 = (f32[2,3,8,1024]{3,0,2,1:T(2,128)S(1)}, f32[2,3,8,1024]{3,0,2,1:T(2,128)S(1)}, u32[]{:S(2)}, u32[]{:S(2)}) collective-permute-start(f32[2,3,8,1024]{3,0,2,1:T(2,128)S(1)} %pad_maximum_fusion.3), channel_id=1, source_target_pairs={{0,24},{8,32},{16,40},{24,48},{32,56},{40,64},{48,72},{56,80},{64,... | collective-permute-start | bytes 589832 | tf_op jit(solution)/shard_map/ppermute | solution.py:28
  57.5 16.5 %collective-permute-start.5 = (f32[2,3,8,1024]{3,0,2,1:T(2,128)S(1)}, f32[2,3,8,1024]{3,0,2,1:T(2,128)S(1)}, u32[]{:S(2)}, u32[]{:S(2)}) collective-permute-start(f32[2,3,8,1024]{3,0,2,1:T(2,128)S(1)} %pad_maximum_fusion.3), channel_id=1, source_target_pairs={{0,16},{8,24},{16,32},{24,40},{32,48},{40,56},{48,64},{56,72},{64,... | collective-permute-start | bytes 589832 | tf_op jit(solution)/shard_map/ppermute | solution.py:28
  61.9 14.0 %collective-permute-start.6 = (f32[2,3,8,1024]{3,0,2,1:T(2,128)S(1)}, f32[2,3,8,1024]{3,0,2,1:T(2,128)S(1)}, u32[]{:S(2)}, u32[]{:S(2)}) collective-permute-start(f32[2,3,8,1024]{3,0,2,1:T(2,128)S(1)} %pad_maximum_fusion.3), channel_id=1, source_target_pairs={{0,8},{8,16},{16,24},{24,32},{32,40},{40,48},{48,56},{56,64},{64,7... | collective-permute-start | bytes 589832 | tf_op jit(solution)/shard_map/ppermute | solution.py:28
  65.6 12.8 %collective-permute-start.7 = (f32[2,3,8,1024]{3,0,2,1:T(2,128)S(1)}, f32[2,3,8,1024]{3,0,2,1:T(2,128)S(1)}, u32[]{:S(2)}, u32[]{:S(2)}) collective-permute-start(f32[2,3,8,1024]{3,0,2,1:T(2,128)S(1)} %pad_maximum_fusion.3), channel_id=1, source_target_pairs={{8,0},{16,8},{24,16},{32,24},{40,32},{48,40},{56,48},{64,56},{72,6... | collective-permute-start | bytes 589832 | tf_op jit(solution)/shard_map/ppermute | solution.py:28
  67.6 12.9 %collective-permute-start.8 = (f32[2,3,8,1024]{3,0,2,1:T(2,128)S(1)}, f32[2,3,8,1024]{3,0,2,1:T(2,128)S(1)}, u32[]{:S(2)}, u32[]{:S(2)}) collective-permute-start(f32[2,3,8,1024]{3,0,2,1:T(2,128)S(1)} %pad_maximum_fusion.3), channel_id=1, source_target_pairs={{16,0},{24,8},{32,16},{40,24},{48,32},{56,40},{64,48},{72,56},{80,... | collective-permute-start | bytes 589832 | tf_op jit(solution)/shard_map/ppermute | solution.py:28
  70.4 10.5 %collective-permute-start.9 = (f32[2,3,8,1024]{3,0,2,1:T(2,128)S(1)}, f32[2,3,8,1024]{3,0,2,1:T(2,128)S(1)}, u32[]{:S(2)}, u32[]{:S(2)}) collective-permute-start(f32[2,3,8,1024]{3,0,2,1:T(2,128)S(1)} %pad_maximum_fusion.3), channel_id=1, source_target_pairs={{24,0},{32,8},{40,16},{48,24},{56,32},{64,40},{72,48},{80,56},{88,... | collective-permute-start | bytes 589832 | tf_op jit(solution)/shard_map/ppermute | solution.py:28
  73.9 8.4 %collective-permute-start.10 = (f32[2,3,8,1024]{3,0,2,1:T(2,128)S(1)}, f32[2,3,8,1024]{3,0,2,1:T(2,128)S(1)}, u32[]{:S(2)}, u32[]{:S(2)}) collective-permute-start(f32[2,3,8,1024]{3,0,2,1:T(2,128)S(1)} %pad_maximum_fusion.3), channel_id=1, source_target_pairs={{32,0},{40,8},{48,16},{56,24},{64,32},{72,40},{80,48},{88,56},{96,... | collective-permute-start | bytes 589832 | tf_op jit(solution)/shard_map/ppermute | solution.py:28
  75.9 24.9 %collective-permute-start.11 = (f32[2,3,8,1024]{3,0,2,1:T(2,128)S(1)}, f32[2,3,8,1024]{3,0,2,1:T(2,128)S(1)}, u32[]{:S(2)}, u32[]{:S(2)}) collective-permute-start(f32[2,3,8,1024]{3,0,2,1:T(2,128)S(1)} %pad_maximum_fusion.3), channel_id=1, source_target_pairs={{40,0},{48,8},{56,16},{64,24},{72,32},{80,40},{88,48},{96,56},{104... | collective-permute-start | bytes 589832 | tf_op jit(solution)/shard_map/ppermute | solution.py:28
  100.8 5.1 %copy-start.5 = (f32[8]{0:T(128)S(1)}, f32[8]{0:T(128)}, u32[]{:S(2)}) copy-start(f32[8]{0:T(128)} %get-tuple-element.9) | copy-start | bytes 100
  100.8 5.1 %copy-start.6 = (pred[8]{0:T(512)(128)(4,1)S(1)}, pred[8]{0:T(512)(128)(4,1)}, u32[]{:S(2)}) copy-start(pred[8]{0:T(512)(128)(4,1)} %get-tuple-element.68) | copy-start | bytes 28
  113.0 12.3 %copy-start.4 = (f32[8]{0:T(128)S(1)}, f32[8]{0:T(128)}, u32[]{:S(2)}) copy-start(f32[8]{0:T(128)} %get-tuple-element.8) | copy-start | bytes 100
  114.2 15.7 %copy-start.3 = (f32[8]{0:T(128)S(1)}, f32[8]{0:T(128)}, u32[]{:S(2)}) copy-start(f32[8]{0:T(128)} %get-tuple-element.7) | copy-start | bytes 100
  147.3 0.7 copy-start.2
where the time goes:
time: 150 us; the launch traced here: 149 us
  local copies, waits for them, and re-layouts  46.9 us (31%)
  starting transfers between devices  38.7 us (26%)
  other arithmetic  32.7 us (22%)
  waiting for transfers between devices  22.5 us (15%)
  between operations  8.14 us (5%)
    ppermute x10, starting transfers between devices, shifted(): return lax.ppermute(x, axis, pairs)  33 us
    ppermute x10, waiting for transfers between devices, shifted(): return lax.ppermute(x, axis, pairs)  22.5 us
    gather x8, local copies, waits for them, and re-layouts, fetch_strip(): return jnp.take(portion, row_index, axis=2) * present  9.8 us
    add x1, other arithmetic, smooth(): across = addend if across is None else across + addend  6.83 us
    slice x2, local copies, waits for them, and re-layouts, cut_strips(): east_strip = blocks[..., :, blocks.shape[-1] - half_width:]  6.37 us
    mul x8, other arithmetic, fetch_strip(): return jnp.take(portion, row_index, axis=2) * present  5.34 us
    add x1, other arithmetic, smooth(): downward = addend if downward is None else downward + addend  4.8 us
    reshape x1, local copies, waits for them, and re-layouts, frame(): east_face = fetch_strip(0, 1).reshape(leading + (block_side, half_width))  4.59 us
  transfers between devices with their start and end apart: 12, of which 5 were waited for; matrix products, arithmetic and copies ran while one was open for 7% of the time, Pallas kernels for 0%

commit v1 on v0

v1 whole, which is shorter than its diff:
```python
import functools

import jax
import jax.numpy as jnp
from jax import lax
from jax.experimental import pallas as pl
from jax.experimental.pallas import tpu as pltpu
from jax.sharding import PartitionSpec as P

MESH = pl.DeviceIdType.MESH
REACH = 4
SLOTS = 8
DAYS = 3
SERIES = 2 * DAYS
TILES = 32
ROWS = TILES * SLOTS
STEP = 4
CHUNKS = (TILES - 4) // STEP
NONE = -(1 << 20)

EAST, WEST, NORTH, SOUTH, NE, NW, SE, SW = range(8)
PLACES = ((1, 0), (-1, 0), (1, -1), (-1, -1), (1, 1), (-1, 1))
OPPOSITE = (1, 0, 5, 4, 3, 2)


def kernel(
    x_hbm, nbr, act, time_taps, space_taps, factor, out_hbm,
    own, left, right, pack, pack_left, pack_right, pack_mixed, packs,
    mixed, strip_n, strip_s, halo, across, swapped, done,
    in_mask, north_mask, north_side, south_mask, south_side, edge_mask, pack_mask, live_mask,
    load_sem, y_send, y_recv, z_send, z_recv, p_send, p_recv, out_sem,
):
    f32 = jnp.float32
    blk, day = lax.axis_index("blk"), lax.axis_index("day")
    blks, days = lax.axis_size("blk"), lax.axis_size("day")
    col, row, rows = blk % REACH, blk // REACH, blks // REACH

    has_left, has_right = day > 0, day < days - 1
    has_north, has_south = row > 0, row < rows - 1

    def place_exists(dx, dz):
        ok = (col + dx >= 0) & (col + dx < REACH)
        if dz:
            ok = ok & (row + dz >= 0) & (row + dz < rows)
        return ok

    partners = [(has_left, 0, -1), (has_right, 0, 1), (has_north, -REACH, 0), (has_south, REACH, 0)]
    for dx, dz in PLACES:
        partners.append((place_exists(dx, dz), dx + REACH * dz, 0))

    load = pltpu.make_async_copy(x_hbm, own, load_sem)
    load.start()
    barrier = pltpu.get_barrier_semaphore()
    expected = 0
    for there, db, dd in partners:
        @pl.when(there)
        def _(db=db, dd=dd):
            pl.semaphore_signal(
                barrier, inc=1, device_id={"blk": blk + db, "day": day + dd}, device_id_type=MESH
            )
        expected = expected + there.astype(jnp.int32)

    lane = lax.broadcasted_iota(jnp.int32, (SLOTS, 128), 1)
    cell = lane & 63
    low, high = cell < 4, cell >= 60
    slot = lax.broadcasted_iota(jnp.int32, (SLOTS, 128), 0)

    def named(direction):
        column = jnp.broadcast_to(nbr[:, direction : direction + 1], (SLOTS, 128))
        return jnp.where(column < 0, NONE, column)

    def on(target, db):
        first = (blk + db) * SLOTS
        return (target >= first) & (target < first + SLOTS)

    def sides(east, west):
        return jnp.where(low, named(east), jnp.where(high, named(west), NONE))

    def picks(ref, target, db):
        first = (blk + db) * SLOTS
        for s in range(SLOTS):
            ref[s] = jnp.where(target == first + s, 1.0, 0.0).astype(f32)

    picks(in_mask, sides(EAST, WEST), 0)
    picks(north_mask, named(NORTH), -REACH)
    picks(north_side, sides(NE, NW), -REACH)
    picks(south_mask, named(SOUTH), REACH)
    picks(south_side, sides(SE, SW), REACH)
    for index, (east, west, dz) in enumerate(((EAST, WEST, 0), (NE, NW, -1), (SE, SW, 1))):
        there = (low & on(named(east), REACH * dz + 1)) | (high & on(named(west), REACH * dz - 1))
        edge_mask[index] = jnp.where(there, 1.0, 0.0).astype(f32)
    at_east = on(named(EAST), 1) | on(named(NE), 1 - REACH) | on(named(SE), 1 + REACH)
    at_west = on(named(WEST), -1) | on(named(NW), -1 - REACH) | on(named(SW), -1 + REACH)
    pack_mask[...] = jnp.where((high & at_east) | (low & at_west), 1.0, 0.0).astype(f32)
    live = jnp.zeros((SLOTS, 128), f32)
    for s in range(SLOTS):
        live = jnp.where(slot == s, act[s].astype(f32), live)
    live_mask[...] = live

    load.wait()

    for t in range(DAYS):
        total = jnp.zeros((SLOTS, 128), f32)
        for c in range(2):
            for q in range(4):
                part = jnp.zeros((SLOTS, 128), f32)
                for s in range(SLOTS):
                    part = part + (
                        own[c * DAYS + t, pl.ds(q * SLOTS + s, SLOTS, stride=4 * SLOTS), :]
                        * pack_mask[s : s + 1, :]
                    )
                shift = 8 * (4 * c + q)
                total = total + (pltpu.roll(part, shift, 1) if shift else part)
        pack[t * SLOTS : (t + 1) * SLOTS, :] = total

    @pl.when(jnp.logical_not(has_left))
    def _():
        pack_left[...] = jnp.zeros_like(pack_left)

        def clear(i, carry):
            left[i] = jnp.zeros((ROWS, 128), f32)
            return carry

        lax.fori_loop(0, SERIES, clear, 0)

    @pl.when(jnp.logical_not(has_right))
    def _():
        pack_right[...] = jnp.zeros_like(pack_right)

        def clear(i, carry):
            right[i] = jnp.zeros((ROWS, 128), f32)
            return carry

        lax.fori_loop(0, SERIES, clear, 0)

    @pl.when(jnp.logical_not(has_north))
    def _():
        strip_n[...] = jnp.zeros_like(strip_n)

    @pl.when(jnp.logical_not(has_south))
    def _():
        strip_s[...] = jnp.zeros_like(strip_s)

    for index, (dx, dz) in enumerate(PLACES):
        @pl.when(jnp.logical_not(place_exists(dx, dz)))
        def _(index=index):
            packs[index] = jnp.zeros((DAYS * SLOTS, 128), f32)

    pl.semaphore_wait(barrier, expected)

    def y_copy(side, item):
        target = left if side == 0 else right
        if isinstance(item, int) and item == 0:
            source, target = pack, (pack_left if side == 0 else pack_right)
        else:
            if isinstance(item, int):
                span = pl.ds(0 if item == 1 else ROWS - 16, 16)
            else:
                span = pl.ds(pl.multiple_of(16 + (item - 3) * (STEP * SLOTS), 8), STEP * SLOTS)
            source, target = x_hbm.at[:, span, :], target.at[:, span, :]
        return pltpu.make_async_remote_copy(
            src_ref=source, dst_ref=target,
            send_sem=y_send.at[side, item], recv_sem=y_recv.at[side, item],
            device_id={"blk": blk, "day": day + (1 if side == 0 else -1)}, device_id_type=MESH,
        )

    for side, there in ((0, has_right), (1, has_left)):
        @pl.when(there)
        def _(side=side):
            for item in range(3):
                y_copy(side, item).start()

            def send(j, carry):
                y_copy(side, j).start()
                return carry

            lax.fori_loop(3, 3 + CHUNKS, send, 0)

    def y_wait(item):
        for side, there in ((0, has_left), (1, has_right)):
            @pl.when(there)
            def _(side=side):
                y_copy(side, item).wait_recv()

    w = [time_taps[k] for k in range(DAYS + 1)]
    a = [space_taps[0, k] for k in range(5)]
    d = [space_taps[1, k] for k in range(5)]
    k00 = factor[0, 0] * factor[0, 0] + factor[0, 1] * factor[0, 1]
    k01 = factor[0, 0] * factor[1, 0] + factor[0, 1] * factor[1, 1]
    k11 = factor[1, 0] * factor[1, 0] + factor[1, 1] * factor[1, 1]

    def filtered(v):
        return [
            w[0] * v[t + 3] + w[1] * (v[t + 2] + v[t + 4])
            + w[2] * (v[t + 1] + v[t + 5]) + w[3] * (v[t] + v[t + 6])
            for t in range(DAYS)
        ]

    def mix_tile(at):
        span = pl.ds(at, SLOTS)
        f = []
        for c in range(2):
            v = [ref[c * DAYS + t, span, :] for ref in (left, own, right) for t in range(DAYS)]
            f.append(filtered(v))
        m = live_mask[...]
        for t in range(DAYS):
            mixed[t, span, :] = (k00 * f[0][t] + k01 * f[1][t]) * m
            mixed[DAYS + t, span, :] = (k01 * f[0][t] + k11 * f[1][t]) * m

    for item in range(3):
        y_wait(item)
    v = [
        ref[t * SLOTS : (t + 1) * SLOTS, :]
        for ref in (pack_left, pack, pack_right) for t in range(DAYS)
    ]
    second = (((lane + 68) >> 3) & 7) >= 4
    for t, f in enumerate(filtered(v)):
        first_part = k00 * f + k01 * pltpu.roll(f, 96, 1)
        second_part = k11 * f + k01 * pltpu.roll(f, 32, 1)
        pack_mixed[t * SLOTS : (t + 1) * SLOTS, :] = jnp.where(second, second_part, first_part)
    for tile in (0, 1, TILES - 2, TILES - 1):
        mix_tile(tile * SLOTS)

    def p_copy(index):
        dx, dz = PLACES[index]
        return pltpu.make_async_remote_copy(
            src_ref=pack_mixed, dst_ref=packs.at[OPPOSITE[index]],
            send_sem=p_send.at[index], recv_sem=p_recv.at[OPPOSITE[index]],
            device_id={"blk": blk + dx + REACH * dz, "day": day}, device_id_type=MESH,
        )

    def p_arrival(index):
        return pltpu.make_async_remote_copy(
            src_ref=pack_mixed, dst_ref=packs.at[index],
            send_sem=p_send.at[index], recv_sem=p_recv.at[index],
            device_id={"blk": blk, "day": day}, device_id_type=MESH,
        )

    def z_copy(side):
        span = pl.ds(ROWS - 16, 16) if side == 0 else pl.ds(0, 16)
        return pltpu.make_async_remote_copy(
            src_ref=mixed.at[:, span, :], dst_ref=strip_n if side == 0 else strip_s,
            send_sem=z_send.at[side], recv_sem=z_recv.at[side],
            device_id={"blk": blk + (REACH if side == 0 else -REACH), "day": day},
            device_id_type=MESH,
        )

    for index, (dx, dz) in enumerate(PLACES):
        @pl.when(place_exists(dx, dz))
        def _(index=index):
            p_copy(index).start()

    for side, there in ((0, has_south), (1, has_north)):
        @pl.when(there)
        def _(side=side):
            z_copy(side).start()

    for index, (dx, dz) in enumerate(PLACES):
        @pl.when(place_exists(dx, dz))
        def _(index=index):
            p_arrival(index).wait_recv()

    for side, there in ((0, has_north), (1, has_south)):
        @pl.when(there)
        def _(side=side):
            z_copy(side).wait_recv()

    west_lanes = (lane & 7) < 4
    for t in range(DAYS):
        span = slice(t * SLOTS, (t + 1) * SLOTS)
        for index in range(3):
            both = jnp.where(west_lanes, packs[2 * index, span, :], packs[2 * index + 1, span, :])
            for c in range(2):
                for q in range(4):
                    shift = 8 * (4 * c + q)
                    value = pltpu.roll(both, 128 - shift, 1) if shift else both
                    halo[index, c * DAYS + t, q] = value

    def pick(ref, series, at, masks):
        total = None
        for s in range(SLOTS):
            term = ref[series, pl.ds(at + s, 1), :] * masks[s]
            total = term if total is None else total + term
        return total

    def filter_across(centre, side, series, at):
        turned = pltpu.roll(side, 64, 1)
        total = a[0] * centre
        for k in range(1, 5):
            ahead = pltpu.roll(jnp.where(cell < k, turned, centre), 128 - k, 1)
            behind = pltpu.roll(jnp.where(cell >= 64 - k, turned, centre), k, 1)
            total = total + a[k] * (ahead + behind)
        span = pl.ds(at, SLOTS)
        across[series, span, :] = total
        swapped[series, span, :] = pltpu.roll(total, 64, 1)

    def own_across(series, tile, g, q):
        at = tile * SLOTS
        side = pick(mixed, series, at, in_mask)
        side = side + halo[0, series, q, pl.ds(g, 1), :] * edge_mask[0]
        filter_across(mixed[series, pl.ds(at, SLOTS), :], side, series, at + 2 * SLOTS)

    def edges_across(series, carry):
        for tile in (0, 1, TILES - 2, TILES - 1):
            own_across(series, tile, tile // 4, tile % 4)
        for n in range(2):
            tile = TILES - 2 + n
            centre = pick(strip_n, series, n * SLOTS, north_mask)
            side = pick(strip_n, series, n * SLOTS, north_side)
            side = side + halo[1, series, tile % 4, pl.ds(tile // 4, 1), :] * edge_mask[1]
            filter_across(centre, side, series, n * SLOTS)
            centre = pick(strip_s, series, n * SLOTS, south_mask)
            side = pick(strip_s, series, n * SLOTS, south_side)
            side = side + halo[2, series, n, pl.ds(0, 1), :] * edge_mask[2]
            filter_across(centre, side, series, (TILES + 2 + n) * SLOTS)
        return carry

    lax.fori_loop(0, SERIES, edges_across, 0)

    first_half = lane < 64

    def filter_down(series, tile):
        base = tile * SLOTS
        m = live_mask[...]
        s = [across[series, pl.ds(base + SLOTS * n, SLOTS), :] for n in range(STEP + 4)]
        b = [swapped[series, pl.ds(base + SLOTS * n, SLOTS), :] for n in range(STEP + 4)]
        o = [jnp.where(first_half, b[n], b[n + 1]) for n in range(STEP + 3)]
        for n in range(STEP):
            total = (
                d[0] * s[n + 2] + d[1] * (o[n + 2] + o[n + 1]) + d[2] * (s[n + 3] + s[n + 1])
                + d[3] * (o[n + 3] + o[n]) + d[4] * (s[n + 4] + s[n])
            )
            done[series, pl.ds(base + SLOTS * n, SLOTS), :] = total * m

    def out_copy(chunk):
        span = pl.ds(pl.multiple_of(chunk * (STEP * SLOTS), 8), STEP * SLOTS)
        return pltpu.make_async_copy(
            done.at[:, span, :], out_hbm.at[:, span, :], out_sem.at[chunk]
        )

    def bulk(j, carry):
        y_wait(j + 3)
        first = pl.multiple_of(16 + j * (STEP * SLOTS), 8)
        for n in range(STEP):
            mix_tile(first + n * SLOTS)

        def series_step(series, inner):
            for n in range(STEP):
                own_across(series, 2 + j * STEP + n, j + (2 + n) // 4, (2 + n) % 4)
            filter_down(series, j * STEP)
            return inner

        lax.fori_loop(0, SERIES, series_step, 0)
        out_copy(j).start()
        return carry

    lax.fori_loop(0, CHUNKS, bulk, 0)

    def last_step(series, carry):
        filter_down(series, TILES - STEP)
        return carry

    lax.fori_loop(0, SERIES, last_step, 0)
    out_copy(CHUNKS).start()

    for side, there in ((0, has_right), (1, has_left)):
        @pl.when(there)
        def _(side=side):
            for item in range(3):
                y_copy(side, item).wait_send()

            def sent(j, carry):
                y_copy(side, j).wait_send()
                return carry

            lax.fori_loop(3, 3 + CHUNKS, sent, 0)

    for index, (dx, dz) in enumerate(PLACES):
        @pl.when(place_exists(dx, dz))
        def _(index=index):
            p_copy(index).wait_send()

    for side, there in ((0, has_south), (1, has_north)):
        @pl.when(there)
        def _(side=side):
            z_copy(side).wait_send()

    def written(chunk, carry):
        out_copy(chunk).wait()
        return carry

    lax.fori_loop(0, CHUNKS + 1, written, 0)


def shards(input_field, active_mask, neighbours, time_taps, space_taps, coregion_factor):
    shape = input_field.shape
    tiles = input_field.reshape(2, DAYS, SLOTS, TILES, 128).transpose(0, 1, 3, 2, 4)
    tiles = tiles.reshape(SERIES, ROWS, 128)
    f32 = jnp.float32
    vmem = pltpu.VMEM
    smem = pl.BlockSpec(memory_space=pltpu.SMEM)
    dma = pltpu.SemaphoreType.DMA
    out = pl.pallas_call(
        kernel,
        out_shape=jax.ShapeDtypeStruct((SERIES, ROWS, 128), f32),
        in_specs=[
            pl.BlockSpec(memory_space=pl.ANY),
            pl.BlockSpec(memory_space=pltpu.VMEM),
            smem, smem, smem, smem,
        ],
        out_specs=pl.BlockSpec(memory_space=pl.ANY),
        scratch_shapes=[
            vmem((SERIES, ROWS, 128), f32),
            vmem((SERIES, ROWS, 128), f32),
            vmem((SERIES, ROWS, 128), f32),
            vmem((DAYS * SLOTS, 128), f32),
            vmem((DAYS * SLOTS, 128), f32),
            vmem((DAYS * SLOTS, 128), f32),
            vmem((DAYS * SLOTS, 128), f32),
            vmem((6, DAYS * SLOTS, 128), f32),
            vmem((SERIES, ROWS, 128), f32),
            vmem((SERIES, 16, 128), f32),
            vmem((SERIES, 16, 128), f32),
            vmem((3, SERIES, 4, SLOTS, 128), f32),
            vmem((SERIES, ROWS + 32, 128), f32),
            vmem((SERIES, ROWS + 32, 128), f32),
            vmem((SERIES, ROWS, 128), f32),
            vmem((SLOTS, SLOTS, 128), f32),
            vmem((SLOTS, SLOTS, 128), f32),
            vmem((SLOTS, SLOTS, 128), f32),
            vmem((SLOTS, SLOTS, 128), f32),
            vmem((SLOTS, SLOTS, 128), f32),
            vmem((3, SLOTS, 128), f32),
            vmem((SLOTS, 128), f32),
            vmem((SLOTS, 128), f32),
            dma,
            dma((2, 3 + CHUNKS)),
            dma((2, 3 + CHUNKS)),
            dma((2,)),
            dma((2,)),
            dma((6,)),
            dma((6,)),
            dma((CHUNKS + 1,)),
        ],
        compiler_params=pltpu.CompilerParams(collective_id=0, has_side_effects=True),
    )(tiles, neighbours, active_mask, time_taps, space_taps, coregion_factor)
    out = out.reshape(2, DAYS, TILES, SLOTS, 128).transpose(0, 1, 3, 2, 4)
    return out.reshape(shape)


def solution(mesh):
    in_specs = (P(None, "day", "blk", None), P("blk"), P("blk", None), P(), P(), P())
    out_specs = P(None, "day", "blk", None)
    return jax.shard_map(shards, mesh=mesh, in_specs=in_specs, out_specs=out_specs, check_vma=False)
```

time: 150 us -> 30.9 us (0.21)
  the two profiles are of different devices: /device:TPU:71 before, /device:TPU:73 now
where the time goes in v1:
time: 30.9 us; the launch traced here: 30.7 us
  Pallas kernels  28.6 us (93%)
  local copies, waits for them, and re-layouts  2.06 us (7%)
    pallas_call x1, Pallas kernels, shards(): pl.pallas_call(kernel, out_shape=jax.ShapeDtypeStruct((SERIES, ROWS, 128)...  28.6 us
    unnamed x1, local copies, waits for them, and re-layouts  2.06 us

profile of v1, /device:TPU:73, one launch (start us, length us, event | category | flops | bytes accessed | tf_op | source)
XLA Modules:
  0.0 30.7 jit_solution(10836852362155438744)
XLA Ops:
  0.0 28.6 %shard_map.64 = f32[6,256,128]{2,1,0:T(8,128)} custom-call(f32[6,256,128]{2,1,0:T(8,128)} %bitcast.11, s32[8,8]{1,0:T(8,128)} %nbr.1, s32[8]{0:T(128)} %act.1, f32[4]{0:T(128)} %time_taps.1, f32[2,5]{1,0:T(2,128)} %space_taps.1, f32[2,2]{1,0:T(2,128)} %factor.1), custom_call_target="tpu_custom_call" | custom-call | tf_op jit(solution)/shard_map/pallas_call | solution.py:403
  28.6 2.1 %copy.8 = f32[2,3,8,4096]{3,2,1,0:T(8,128)} copy(f32[2,3,8,4096]{3,2,1,0:T(8,128)} %bitcast.10) | data formatting | bytes 1572864

commit v2 on v1

--- a/solution.py
+++ b/solution.py
@@ -16,6 +16,7 @@
 ROWS = TILES * SLOTS
 STEP = 4
 CHUNKS = (TILES - 4) // STEP
+AHEAD = 1
 NONE = -(1 << 20)
 
 EAST, WEST, NORTH, SOUTH, NE, NW, SE, SW = range(8)
@@ -26,11 +27,11 @@
 def kernel(
     x_hbm, nbr, act, time_taps, space_taps, factor, out_hbm,
     own, left, right, pack, pack_left, pack_right, pack_mixed, packs,
-    mixed, strip_n, strip_s, halo, across, swapped, done,
-    in_mask, north_mask, north_side, south_mask, south_side, edge_mask, pack_mask, live_mask,
+    mixed, strip_n, strip_s, halo, lhs, weights, across, swapped, done,
+    take_index, take_mask, edge_mask, live_mask,
     load_sem, y_send, y_recv, z_send, z_recv, p_send, p_recv, out_sem,
 ):
-    f32 = jnp.float32
+    f32, bf16 = jnp.float32, jnp.bfloat16
     blk, day = lax.axis_index("blk"), lax.axis_index("day")
     blks, days = lax.axis_size("blk"), lax.axis_size("day")
     col, row, rows = blk % REACH, blk // REACH, blks // REACH
@@ -76,43 +77,28 @@
     def sides(east, west):
         return jnp.where(low, named(east), jnp.where(high, named(west), NONE))
 
-    def picks(ref, target, db):
-        first = (blk + db) * SLOTS
-        for s in range(SLOTS):
-            ref[s] = jnp.where(target == first + s, 1.0, 0.0).astype(f32)
-
-    picks(in_mask, sides(EAST, WEST), 0)
-    picks(north_mask, named(NORTH), -REACH)
-    picks(north_side, sides(NE, NW), -REACH)
-    picks(south_mask, named(SOUTH), REACH)
-    picks(south_side, sides(SE, SW), REACH)
+    for index, (target, db) in enumerate((
+        (sides(EAST, WEST), 0),
+        (named(NORTH), -REACH), (sides(NE, NW), -REACH),
+        (named(SOUTH), REACH), (sides(SE, SW), REACH),
+    )):
+        take_index[index] = target & (SLOTS - 1)
+        take_mask[index] = jnp.where(on(target, db), 1.0, 0.0).astype(f32)
     for index, (east, west, dz) in enumerate(((EAST, WEST, 0), (NE, NW, -1), (SE, SW, 1))):
         there = (low & on(named(east), REACH * dz + 1)) | (high & on(named(west), REACH * dz - 1))
         edge_mask[index] = jnp.where(there, 1.0, 0.0).astype(f32)
     at_east = on(named(EAST), 1) | on(named(NE), 1 - REACH) | on(named(SE), 1 + REACH)
     at_west = on(named(WEST), -1) | on(named(NW), -1 - REACH) | on(named(SW), -1 + REACH)
-    pack_mask[...] = jnp.where((high & at_east) | (low & at_west), 1.0, 0.0).astype(f32)
+    ends = jnp.where((high & at_east) | (low & at_west), 1.0, 0.0).astype(f32)
+    end_slot = jnp.broadcast_to(
+        jnp.sum(ends * slot.astype(f32), axis=0, keepdims=True), (SLOTS, 128)
+    ).astype(jnp.int32)
+    end_mask = jnp.broadcast_to(jnp.sum(ends, axis=0, keepdims=True), (SLOTS, 128))
     live = jnp.zeros((SLOTS, 128), f32)
     for s in range(SLOTS):
         live = jnp.where(slot == s, act[s].astype(f32), live)
     live_mask[...] = live
 
-    load.wait()
-
-    for t in range(DAYS):
-        total = jnp.zeros((SLOTS, 128), f32)
-        for c in range(2):
-            for q in range(4):
-                part = jnp.zeros((SLOTS, 128), f32)
-                for s in range(SLOTS):
-                    part = part + (
-                        own[c * DAYS + t, pl.ds(q * SLOTS + s, SLOTS, stride=4 * SLOTS), :]
-                        * pack_mask[s : s + 1, :]
-                    )
-                shift = 8 * (4 * c + q)
-                total = total + (pltpu.roll(part, shift, 1) if shift else part)
-        pack[t * SLOTS : (t + 1) * SLOTS, :] = total
-
     @pl.when(jnp.logical_not(has_left))
     def _():
         pack_left[...] = jnp.zeros_like(pack_left)
@@ -147,16 +133,20 @@
             packs[index] = jnp.zeros((DAYS * SLOTS, 128), f32)
 
     pl.semaphore_wait(barrier, expected)
+
+    def bulk_row(j):
+        at = 16 + j * (STEP * SLOTS)
+        return at if isinstance(j, int) else pl.multiple_of(at, 8)
 
     def y_copy(side, item):
         target = left if side == 0 else right
         if isinstance(item, int) and item == 0:
             source, target = pack, (pack_left if side == 0 else pack_right)
         else:
-            if isinstance(item, int):
+            if isinstance(item, int) and item < 3:
                 span = pl.ds(0 if item == 1 else ROWS - 16, 16)
             else:
-                span = pl.ds(pl.multiple_of(16 + (item - 3) * (STEP * SLOTS), 8), STEP * SLOTS)
+                span = pl.ds(bulk_row(item - 3), STEP * SLOTS)
             source, target = x_hbm.at[:, span, :], target.at[:, span, :]
         return pltpu.make_async_remote_copy(
             src_ref=source, dst_ref=target,
@@ -167,14 +157,35 @@
     for side, there in ((0, has_right), (1, has_left)):
         @pl.when(there)
         def _(side=side):
-            for item in range(3):
+            for item in range(1, 3 + AHEAD):
                 y_copy(side, item).start()
+
+    load.wait()
+
+    for t in range(DAYS):
+        total = jnp.zeros((SLOTS, 128), f32)
+        for c in range(2):
+            for q in range(4):
+                part = None
+                for g in range(SLOTS):
+                    value = own[c * DAYS + t, pl.ds((4 * g + q) * SLOTS, SLOTS), :]
+                    value = jnp.take_along_axis(value, end_slot, axis=0)
+                    part = value if part is None else jnp.where(slot == g, value, part)
+                part = part * end_mask
+                shift = 8 * (4 * c + q)
+                total = total + (pltpu.roll(part, shift, 1) if shift else part)
+        pack[t * SLOTS : (t + 1) * SLOTS, :] = total
+
+    for side, there in ((0, has_right), (1, has_left)):
+        @pl.when(there)
+        def _(side=side):
+            y_copy(side, 0).start()
 
             def send(j, carry):
                 y_copy(side, j).start()
                 return carry
 
-            lax.fori_loop(3, 3 + CHUNKS, send, 0)
+            lax.fori_loop(3 + AHEAD, 3 + CHUNKS, send, 0)
 
     def y_wait(item):
         for side, there in ((0, has_left), (1, has_right)):
@@ -188,6 +199,21 @@
     k00 = factor[0, 0] * factor[0, 0] + factor[0, 1] * factor[0, 1]
     k01 = factor[0, 0] * factor[1, 0] + factor[0, 1] * factor[1, 1]
     k11 = factor[1, 0] * factor[1, 0] + factor[1, 1] * factor[1, 1]
+
+    k = lax.broadcasted_iota(jnp.int32, (256, 256), 0)
+    n = lax.broadcasted_iota(jnp.int32, (256, 256), 1)
+    place = k & 63
+    beyond = jnp.where(place < 4, place + 64, jnp.where(place >= 60, place - 64, 1024))
+    place = jnp.where(k >= 128, beyond, place)
+    distance = jnp.abs(place - (n & 63))
+    same_row = ((k >> 6) & 1) == (((n >> 6) ^ (n >> 7)) & 1)
+    weight = jnp.zeros((256, 256), f32)
+    for tap in range(5):
+        weight = jnp.where(same_row & (distance == tap), a[tap], weight)
+    weight_high = weight.astype(bf16)
+    weights[0:256, :] = weight_high
+    weights[256:512, :] = weight_high
+    weights[512:768, :] = (weight - weight_high.astype(f32)).astype(bf16)
 
     def filtered(v):
         return [
@@ -276,46 +302,59 @@
                     value = pltpu.roll(both, 128 - shift, 1) if shift else both
                     halo[index, c * DAYS + t, q] = value
 
-    def pick(ref, series, at, masks):
-        total = None
-        for s in range(SLOTS):
-            term = ref[series, pl.ds(at + s, 1), :] * masks[s]
-            total = term if total is None else total + term
-        return total
-
-    def filter_across(centre, side, series, at):
-        turned = pltpu.roll(side, 64, 1)
-        total = a[0] * centre
-        for k in range(1, 5):
-            ahead = pltpu.roll(jnp.where(cell < k, turned, centre), 128 - k, 1)
-            behind = pltpu.roll(jnp.where(cell >= 64 - k, turned, centre), k, 1)
-            total = total + a[k] * (ahead + behind)
-        span = pl.ds(at, SLOTS)
-        across[series, span, :] = total
-        swapped[series, span, :] = pltpu.roll(total, 64, 1)
-
-    def own_across(series, tile, g, q):
-        at = tile * SLOTS
-        side = pick(mixed, series, at, in_mask)
-        side = side + halo[0, series, q, pl.ds(g, 1), :] * edge_mask[0]
-        filter_across(mixed[series, pl.ds(at, SLOTS), :], side, series, at + 2 * SLOTS)
-
-    def edges_across(series, carry):
-        for tile in (0, 1, TILES - 2, TILES - 1):
-            own_across(series, tile, tile // 4, tile % 4)
-        for n in range(2):
-            tile = TILES - 2 + n
-            centre = pick(strip_n, series, n * SLOTS, north_mask)
-            side = pick(strip_n, series, n * SLOTS, north_side)
-            side = side + halo[1, series, tile % 4, pl.ds(tile // 4, 1), :] * edge_mask[1]
-            filter_across(centre, side, series, n * SLOTS)
-            centre = pick(strip_s, series, n * SLOTS, south_mask)
-            side = pick(strip_s, series, n * SLOTS, south_side)
-            side = side + halo[2, series, n, pl.ds(0, 1), :] * edge_mask[2]
-            filter_across(centre, side, series, (TILES + 2 + n) * SLOTS)
+    def take(value, index):
+        return jnp.take_along_axis(value, take_index[index], axis=0) * take_mask[index]
+
+    def own_side(series, at, g, q):
+        side = take(mixed[series, pl.ds(at, SLOTS), :], 0)
+        return side + halo[0, series, q, pl.ds(g, 1), :] * edge_mask[0]
+
+    def stage(series, centres, side_tiles):
+        span = pl.ds(pl.multiple_of(series * (STEP * SLOTS), 8), STEP * SLOTS)
+        for column, value in ((0, centres), (128, jnp.concatenate(side_tiles, axis=0))):
+            top = value.astype(bf16)
+            rest = (value - top.astype(f32)).astype(bf16)
+            lhs[span, column : column + 128] = top
+            lhs[span, 256 + column : 384 + column] = rest
+            lhs[span, 512 + column : 640 + column] = top
+
+    def filter_across(at):
+        result = jnp.dot(lhs[...], weights[...], preferred_element_type=f32)
+        for series in range(SERIES):
+            part = result[series * STEP * SLOTS : (series + 1) * STEP * SLOTS]
+            across[series, pl.ds(at, STEP * SLOTS), :] = part[:, :128]
+            swapped[series, pl.ds(at, STEP * SLOTS), :] = part[:, 128:]
+
+    def north_stage(series, carry):
+        centres, side_tiles = [], []
+        for tile in range(2):
+            value = strip_n[series, tile * SLOTS : (tile + 1) * SLOTS, :]
+            centres.append(take(value, 1))
+            edge = halo[1, series, 2 + tile, SLOTS - 1 : SLOTS, :] * edge_mask[1]
+            side_tiles.append(take(value, 2) + edge)
+        for tile in range(2):
+            centres.append(mixed[series, tile * SLOTS : (tile + 1) * SLOTS, :])
+            side_tiles.append(own_side(series, tile * SLOTS, 0, tile))
+        stage(series, jnp.concatenate(centres, axis=0), side_tiles)
         return carry
 
-    lax.fori_loop(0, SERIES, edges_across, 0)
+    def south_stage(series, carry):
+        centres, side_tiles = [], []
+        for tile in range(TILES - 2, TILES):
+            centres.append(mixed[series, tile * SLOTS : (tile + 1) * SLOTS, :])
+            side_tiles.append(own_side(series, tile * SLOTS, SLOTS - 1, tile % 4))
+        for tile in range(2):
+            value = strip_s[series, tile * SLOTS : (tile + 1) * SLOTS, :]
+            centres.append(take(value, 3))
+            edge = halo[2, series, tile, 0:1, :] * edge_mask[2]
+            side_tiles.append(take(value, 4) + edge)
+        stage(series, jnp.concatenate(centres, axis=0), side_tiles)
+        return carry
+
+    lax.fori_loop(0, SERIES, north_stage, 0)
+    filter_across(0)
+    lax.fori_loop(0, SERIES, south_stage, 0)
+    filter_across(ROWS)
 
     first_half = lane < 64
 
@@ -340,17 +379,25 @@
 
     def bulk(j, carry):
         y_wait(j + 3)
-        first = pl.multiple_of(16 + j * (STEP * SLOTS), 8)
+        first = bulk_row(j)
         for n in range(STEP):
             mix_tile(first + n * SLOTS)
 
-        def series_step(series, inner):
-            for n in range(STEP):
-                own_across(series, 2 + j * STEP + n, j + (2 + n) // 4, (2 + n) % 4)
+        def stage_step(series, inner):
+            side_tiles = [
+                own_side(series, first + n * SLOTS, j + (2 + n) // 4, (2 + n) % 4)
+                for n in range(STEP)
+            ]
+            stage(series, mixed[series, pl.ds(first, STEP * SLOTS), :], side_tiles)
+            return inner
+
+        def down_step(series, inner):
             filter_down(series, j * STEP)
             return inner
 
-        lax.fori_loop(0, SERIES, series_step, 0)
+        lax.fori_loop(0, SERIES, stage_step, 0)
+        filter_across(first + 2 * SLOTS)
+        lax.fori_loop(0, SERIES, down_step, 0)
         out_copy(j).start()
         return carry
 
@@ -422,16 +469,14 @@
             vmem((SERIES, 16, 128), f32),
             vmem((SERIES, 16, 128), f32),
             vmem((3, SERIES, 4, SLOTS, 128), f32),
+            vmem((SERIES * STEP * SLOTS, 768), jnp.bfloat16),
+            vmem((768, 256), jnp.bfloat16),
             vmem((SERIES, ROWS + 32, 128), f32),
             vmem((SERIES, ROWS + 32, 128), f32),
             vmem((SERIES, ROWS, 128), f32),
-            vmem((SLOTS, SLOTS, 128), f32),
-            vmem((SLOTS, SLOTS, 128), f32),
-            vmem((SLOTS, SLOTS, 128), f32),
-            vmem((SLOTS, SLOTS, 128), f32),
-            vmem((SLOTS, SLOTS, 128), f32),
+            vmem((5, SLOTS, 128), jnp.int32),
+            vmem((5, SLOTS, 128), f32),
             vmem((3, SLOTS, 128), f32),
-            vmem((SLOTS, 128), f32),
             vmem((SLOTS, 128), f32),
             dma,
             dma((2, 3 + CHUNKS)),

time: 30.9 us -> 23.3 us (0.75)
  Pallas kernels: 28.6 us -> 21 us
    pallas_call x1, Pallas kernels: 28.6 us -> 21 us  [shards(): pl.pallas_call(kernel, out_shape=jax.ShapeDtypeStruct((SERIES, ROWS, 128)...]
where the time goes in v2:
time: 23.3 us; the launch traced here: 23.1 us
  Pallas kernels  21 us (90%)
  local copies, waits for them, and re-layouts  2.06 us (9%)
    pallas_call x1, Pallas kernels, shards(): pl.pallas_call(kernel, out_shape=jax.ShapeDtypeStruct((SERIES, ROWS, 128)...  21 us
    unnamed x1, local copies, waits for them, and re-layouts  2.06 us

profile of v2, /device:TPU:73, one launch (start us, length us, event | category | flops | bytes accessed | tf_op | source)
XLA Modules:
  0.0 23.1 jit_solution(17760209175795801866)
XLA Ops:
  0.0 21.0 %shard_map.64 = f32[6,256,128]{2,1,0:T(8,128)} custom-call(f32[6,256,128]{2,1,0:T(8,128)} %bitcast.11, s32[8,8]{1,0:T(8,128)} %nbr.1, s32[8]{0:T(128)} %act.1, f32[4]{0:T(128)} %time_taps.1, f32[2,5]{1,0:T(2,128)} %space_taps.1, f32[2,2]{1,0:T(2,128)} %factor.1), custom_call_target="tpu_custom_call" | custom-call | tf_op jit(solution)/shard_map/pallas_call | solution.py:450
  21.0 2.1 %copy.8 = f32[2,3,8,4096]{3,2,1,0:T(8,128)} copy(f32[2,3,8,4096]{3,2,1,0:T(8,128)} %bitcast.10) | data formatting | bytes 1572864

commit v3 on v2

--- a/solution.py
+++ b/solution.py
@@ -17,6 +17,7 @@
 STEP = 4
 CHUNKS = (TILES - 4) // STEP
 AHEAD = 1
+EARLY = 4
 NONE = -(1 << 20)
 
 EAST, WEST, NORTH, SOUTH, NE, NW, SE, SW = range(8)
@@ -25,11 +26,12 @@
 
 
 def kernel(
-    x_hbm, nbr, act, time_taps, space_taps, factor, out_hbm,
+    x_hbm, nbr_hbm, act_hbm, time_hbm, space_hbm, factor_hbm, done,
     own, left, right, pack, pack_left, pack_right, pack_mixed, packs,
-    mixed, strip_n, strip_s, halo, lhs, weights, across, swapped, done,
+    mixed, strip_n, strip_s, halo, lhs, weights, across, swapped,
     take_index, take_mask, edge_mask, live_mask,
-    load_sem, y_send, y_recv, z_send, z_recv, p_send, p_recv, out_sem,
+    nbr, act, time_taps, space_taps, factor,
+    load_sem, small_sem, y_send, y_recv, z_send, z_recv, p_send, p_recv,
 ):
     f32, bf16 = jnp.float32, jnp.bfloat16
     blk, day = lax.axis_index("blk"), lax.axis_index("day")
@@ -49,8 +51,6 @@
     for dx, dz in PLACES:
         partners.append((place_exists(dx, dz), dx + REACH * dz, 0))
 
-    load = pltpu.make_async_copy(x_hbm, own, load_sem)
-    load.start()
     barrier = pltpu.get_barrier_semaphore()
     expected = 0
     for there, db, dd in partners:
@@ -60,6 +60,49 @@
                 barrier, inc=1, device_id={"blk": blk + db, "day": day + dd}, device_id_type=MESH
             )
         expected = expected + there.astype(jnp.int32)
+
+    small = [
+        pltpu.make_async_copy(source, target, small_sem.at[index])
+        for index, (source, target) in enumerate((
+            (nbr_hbm, nbr), (act_hbm, act), (time_hbm, time_taps), (space_hbm, space_taps),
+            (factor_hbm, factor),
+        ))
+    ]
+    for copy in small:
+        copy.start()
+    load = pltpu.make_async_copy(x_hbm, own, load_sem)
+    load.start()
+
+    pl.semaphore_wait(barrier, expected)
+
+    def bulk_row(j):
+        at = 16 + j * (STEP * SLOTS)
+        return at if isinstance(j, int) else pl.multiple_of(at, 8)
+
+    def y_copy(side, item):
+        target = left if side == 0 else right
+        if isinstance(item, int) and item == 0:
+            source, target = pack, (pack_left if side == 0 else pack_right)
+        else:
+            if isinstance(item, int) and item < 3:
+                span = pl.ds(0 if item == 1 else ROWS - 16, 16)
+            else:
+                span = pl.ds(bulk_row(item - 3), STEP * SLOTS)
+            source, target = x_hbm.at[:, span, :], target.at[:, span, :]
+        return pltpu.make_async_remote_copy(
+            src_ref=source, dst_ref=target,
+            send_sem=y_send.at[side, item], recv_sem=y_recv.at[side, item],
+            device_id={"blk": blk, "day": day + (1 if side == 0 else -1)}, device_id_type=MESH,
+        )
+
+    for side, there in ((0, has_right), (1, has_left)):
+        @pl.when(there)
+        def _(side=side):
+            for item in range(1, 3 + AHEAD):
+                y_copy(side, item).start()
+
+    for copy in small:
+        copy.wait()
 
     lane = lax.broadcasted_iota(jnp.int32, (SLOTS, 128), 1)
     cell = lane & 63
@@ -132,34 +175,6 @@
         def _(index=index):
             packs[index] = jnp.zeros((DAYS * SLOTS, 128), f32)
 
-    pl.semaphore_wait(barrier, expected)
-
-    def bulk_row(j):
-        at = 16 + j * (STEP * SLOTS)
-        return at if isinstance(j, int) else pl.multiple_of(at, 8)
-
-    def y_copy(side, item):
-        target = left if side == 0 else right
-        if isinstance(item, int) and item == 0:
-            source, target = pack, (pack_left if side == 0 else pack_right)
-        else:
-            if isinstance(item, int) and item < 3:
-                span = pl.ds(0 if item == 1 else ROWS - 16, 16)
-            else:
-                span = pl.ds(bulk_row(item - 3), STEP * SLOTS)
-            source, target = x_hbm.at[:, span, :], target.at[:, span, :]
-        return pltpu.make_async_remote_copy(
-            src_ref=source, dst_ref=target,
-            send_sem=y_send.at[side, item], recv_sem=y_recv.at[side, item],
-            device_id={"blk": blk, "day": day + (1 if side == 0 else -1)}, device_id_type=MESH,
-        )
-
-    for side, there in ((0, has_right), (1, has_left)):
-        @pl.when(there)
-        def _(side=side):
-            for item in range(1, 3 + AHEAD):
-                y_copy(side, item).start()
-
     load.wait()
 
     for t in range(DAYS):
@@ -281,6 +296,14 @@
         def _(side=side):
             z_copy(side).start()
 
+    def mix_chunk(j, carry):
+        y_wait(j + 3)
+        for n in range(STEP):
+            mix_tile(bulk_row(j) + n * SLOTS)
+        return carry
+
+    lax.fori_loop(0, EARLY, mix_chunk, 0)
+
     for index, (dx, dz) in enumerate(PLACES):
         @pl.when(place_exists(dx, dz))
         def _(index=index):
@@ -371,17 +394,8 @@
             )
             done[series, pl.ds(base + SLOTS * n, SLOTS), :] = total * m
 
-    def out_copy(chunk):
-        span = pl.ds(pl.multiple_of(chunk * (STEP * SLOTS), 8), STEP * SLOTS)
-        return pltpu.make_async_copy(
-            done.at[:, span, :], out_hbm.at[:, span, :], out_sem.at[chunk]
-        )
-
-    def bulk(j, carry):
-        y_wait(j + 3)
+    def space_chunk(j, carry):
         first = bulk_row(j)
-        for n in range(STEP):
-            mix_tile(first + n * SLOTS)
 
         def stage_step(series, inner):
             side_tiles = [
@@ -398,17 +412,21 @@
         lax.fori_loop(0, SERIES, stage_step, 0)
         filter_across(first + 2 * SLOTS)
         lax.fori_loop(0, SERIES, down_step, 0)
-        out_copy(j).start()
         return carry
 
-    lax.fori_loop(0, CHUNKS, bulk, 0)
+    lax.fori_loop(0, EARLY, space_chunk, 0)
+
+    def bulk(j, carry):
+        mix_chunk(j, carry)
+        return space_chunk(j, carry)
+
+    lax.fori_loop(EARLY, CHUNKS, bulk, 0)
 
     def last_step(series, carry):
         filter_down(series, TILES - STEP)
         return carry
 
     lax.fori_loop(0, SERIES, last_step, 0)
-    out_copy(CHUNKS).start()
 
     for side, there in ((0, has_right), (1, has_left)):
         @pl.when(there)
@@ -431,12 +449,6 @@
         @pl.when(there)
         def _(side=side):
             z_copy(side).wait_send()
-
-    def written(chunk, carry):
-        out_copy(chunk).wait()
-        return carry
-
-    lax.fori_loop(0, CHUNKS + 1, written, 0)
 
 
 def shards(input_field, active_mask, neighbours, time_taps, space_taps, coregion_factor):
@@ -445,17 +457,12 @@
     tiles = tiles.reshape(SERIES, ROWS, 128)
     f32 = jnp.float32
     vmem = pltpu.VMEM
-    smem = pl.BlockSpec(memory_space=pltpu.SMEM)
     dma = pltpu.SemaphoreType.DMA
     out = pl.pallas_call(
         kernel,
-        out_shape=jax.ShapeDtypeStruct((SERIES, ROWS, 128), f32),
-        in_specs=[
-            pl.BlockSpec(memory_space=pl.ANY),
-            pl.BlockSpec(memory_space=pltpu.VMEM),
-            smem, smem, smem, smem,
-        ],
-        out_specs=pl.BlockSpec(memory_space=pl.ANY),
+        out_shape=vmem((SERIES, ROWS, 128), f32),
+        in_specs=[pl.BlockSpec(memory_space=pl.ANY)] * 6,
+        out_specs=pl.BlockSpec(memory_space=vmem),
         scratch_shapes=[
             vmem((SERIES, ROWS, 128), f32),
             vmem((SERIES, ROWS, 128), f32),
@@ -473,19 +480,23 @@
             vmem((768, 256), jnp.bfloat16),
             vmem((SERIES, ROWS + 32, 128), f32),
             vmem((SERIES, ROWS + 32, 128), f32),
-            vmem((SERIES, ROWS, 128), f32),
             vmem((5, SLOTS, 128), jnp.int32),
             vmem((5, SLOTS, 128), f32),
             vmem((3, SLOTS, 128), f32),
             vmem((SLOTS, 128), f32),
+            vmem((SLOTS, 8), jnp.int32),
+            pltpu.SMEM((SLOTS,), jnp.int32),
+            pltpu.SMEM((DAYS + 1,), f32),
+            pltpu.SMEM((2, 5), f32),
+            pltpu.SMEM((2, 2), f32),
             dma,
+            dma((5,)),
             dma((2, 3 + CHUNKS)),
             dma((2, 3 + CHUNKS)),
             dma((2,)),
             dma((2,)),
             dma((6,)),
             dma((6,)),
-            dma((CHUNKS + 1,)),
         ],
         compiler_params=pltpu.CompilerParams(collective_id=0, has_side_effects=True),
     )(tiles, neighbours, active_mask, time_taps, space_taps, coregion_factor)

time: 23.3 us -> 20.3 us (0.87)
  the two profiles are of different devices: /device:TPU:73 before, /device:TPU:201 now
where the time goes in v3:
time: 20.3 us; the launch traced here: 20.2 us
  Pallas kernels  19.3 us (95%)
  local copies, waits for them, and re-layouts  0.88 us (4%)
    pallas_call x1, Pallas kernels, shards(): pl.pallas_call(kernel, out_shape=vmem((SERIES, ROWS, 128), f32), in_specs...  19.3 us
    unnamed x1, local copies, waits for them, and re-layouts  0.88 us

profile of v3, /device:TPU:201, one launch (start us, length us, event | category | flops | bytes accessed | tf_op | source)
XLA Modules:
  0.0 20.2 jit_solution(2712110605529239809)
XLA Ops:
  0.0 19.3 %shard_map.64 = f32[6,256,128]{2,1,0:T(8,128)S(1)} custom-call(f32[6,256,128]{2,1,0:T(8,128)} %bitcast.11, s32[8,8]{1,0:T(8,128)} %nbr_hbm.1, s32[8]{0:T(128)} %act_hbm.1, f32[4]{0:T(128)} %time_hbm.1, f32[2,5]{1,0:T(2,128)} %space_hbm.1, f32[2,2]{1,0:T(2,128)} %factor_hbm.1), custom_call_target="tpu_custom_call" | custom-call | tf_op jit(solution)/shard_map/pallas_call | solution.py:461
  19.3 0.9 %copy.8 = f32[2,3,8,4096]{3,2,1,0:T(8,128)} copy(f32[2,3,8,4096]{3,2,1,0:T(8,128)S(1)} %bitcast.10) | data formatting | bytes 1572864

commit v4 on v3

--- a/solution.py
+++ b/solution.py
@@ -16,8 +16,8 @@
 ROWS = TILES * SLOTS
 STEP = 4
 CHUNKS = (TILES - 4) // STEP
-AHEAD = 1
-EARLY = 4
+AHEAD = 0
+EARLY = 3
 NONE = -(1 << 20)
 
 EAST, WEST, NORTH, SOUTH, NE, NW, SE, SW = range(8)
@@ -32,6 +32,7 @@
     take_index, take_mask, edge_mask, live_mask,
     nbr, act, time_taps, space_taps, factor,
     load_sem, small_sem, y_send, y_recv, z_send, z_recv, p_send, p_recv,
+    days_ready, edges_ready,
 ):
     f32, bf16 = jnp.float32, jnp.bfloat16
     blk, day = lax.axis_index("blk"), lax.axis_index("day")
@@ -47,19 +48,33 @@
             ok = ok & (row + dz >= 0) & (row + dz < rows)
         return ok
 
-    partners = [(has_left, 0, -1), (has_right, 0, 1), (has_north, -REACH, 0), (has_south, REACH, 0)]
-    for dx, dz in PLACES:
-        partners.append((place_exists(dx, dz), dx + REACH * dz, 0))
-
+    core = day % 2
+    chip = day - core
+    first_core, second_core = core == 0, core == 1
     barrier = pltpu.get_barrier_semaphore()
-    expected = 0
-    for there, db, dd in partners:
-        @pl.when(there)
-        def _(db=db, dd=dd):
+
+    def hello(there, db, to_day):
+        @pl.when(there)
+        def _():
             pl.semaphore_signal(
-                barrier, inc=1, device_id={"blk": blk + db, "day": day + dd}, device_id_type=MESH
+                barrier, inc=1, device_id={"blk": blk + db, "day": to_day}, device_id_type=MESH
             )
-        expected = expected + there.astype(jnp.int32)
+
+    def tell(sem, to_day):
+        pl.semaphore_signal(
+            sem, inc=1, device_id={"blk": blk, "day": to_day}, device_id_type=MESH
+        )
+
+    hello(first_core, 0, day + 1)
+    hello(first_core & has_left, 0, day - 1)
+    hello(second_core & has_right, 0, day + 2)
+    expected_days = 1 + has_right.astype(jnp.int32) + (day > 1).astype(jnp.int32)
+    expected_edges = 0
+    for there, db in [(has_north, -REACH), (has_south, REACH)] + [
+        (place_exists(dx, dz), dx + REACH * dz) for dx, dz in PLACES
+    ]:
+        hello(there, db, chip)
+        expected_edges = expected_edges + 2 * there.astype(jnp.int32)
 
     small = [
         pltpu.make_async_copy(source, target, small_sem.at[index])
@@ -73,7 +88,14 @@
     load = pltpu.make_async_copy(x_hbm, own, load_sem)
     load.start()
 
-    pl.semaphore_wait(barrier, expected)
+    @pl.when(second_core)
+    def _():
+        pl.semaphore_wait(barrier, expected_days)
+        tell(days_ready, day - 1)
+
+    @pl.when(first_core)
+    def _():
+        pl.semaphore_wait(days_ready, 1)
 
     def bulk_row(j):
         at = 16 + j * (STEP * SLOTS)
@@ -285,6 +307,15 @@
             device_id={"blk": blk + (REACH if side == 0 else -REACH), "day": day},
             device_id_type=MESH,
         )
+
+    @pl.when(first_core)
+    def _():
+        pl.semaphore_wait(barrier, expected_edges)
+        tell(edges_ready, day + 1)
+
+    @pl.when(second_core)
+    def _():
+        pl.semaphore_wait(edges_ready, 1)
 
     for index, (dx, dz) in enumerate(PLACES):
         @pl.when(place_exists(dx, dz))
@@ -497,6 +528,8 @@
             dma((2,)),
             dma((6,)),
             dma((6,)),
+            pltpu.SemaphoreType.REGULAR,
+            pltpu.SemaphoreType.REGULAR,
         ],
         compiler_params=pltpu.CompilerParams(collective_id=0, has_side_effects=True),
     )(tiles, neighbours, active_mask, time_taps, space_taps, coregion_factor)

time: 20.3 us -> 18.9 us (0.931)
  the two profiles are of different devices: /device:TPU:201 before, /device:TPU:8 now
where the time goes in v4:
time: 18.9 us; the launch traced here: 18.8 us
  Pallas kernels  17.9 us (95%)
  local copies, waits for them, and re-layouts  0.88 us (5%)
    pallas_call x1, Pallas kernels, shards(): pl.pallas_call(kernel, out_shape=vmem((SERIES, ROWS, 128), f32), in_specs...  17.9 us
    unnamed x1, local copies, waits for them, and re-layouts  0.88 us

profile of v4, /device:TPU:8, one launch (start us, length us, event | category | flops | bytes accessed | tf_op | source)
XLA Modules:
  0.0 18.8 jit_solution(837333180207633838)
XLA Ops:
  0.0 17.9 %shard_map.64 = f32[6,256,128]{2,1,0:T(8,128)S(1)} custom-call(f32[6,256,128]{2,1,0:T(8,128)} %bitcast.11, s32[8,8]{1,0:T(8,128)} %nbr_hbm.1, s32[8]{0:T(128)} %act_hbm.1, f32[4]{0:T(128)} %time_hbm.1, f32[2,5]{1,0:T(2,128)} %space_hbm.1, f32[2,2]{1,0:T(2,128)} %factor_hbm.1), custom_call_target="tpu_custom_call" | custom-call | tf_op jit(solution)/shard_map/pallas_call | solution.py:492
  17.9 0.9 %copy.8 = f32[2,3,8,4096]{3,2,1,0:T(8,128)} copy(f32[2,3,8,4096]{3,2,1,0:T(8,128)S(1)} %bitcast.10) | data formatting | bytes 1572864

commit v5 on v4

--- a/solution.py
+++ b/solution.py
@@ -65,11 +65,13 @@
             sem, inc=1, device_id={"blk": blk, "day": to_day}, device_id_type=MESH
         )
 
-    hello(first_core, 0, day + 1)
+    first_chip = day < 2
+    hello(first_core & ~first_chip, 0, day + 1)
     hello(first_core & has_left, 0, day - 1)
     hello(second_core & has_right, 0, day + 2)
-    expected_days = 1 + has_right.astype(jnp.int32) + (day > 1).astype(jnp.int32)
-    expected_edges = 0
+    hello(second_core & first_chip, 0, day - 1)
+    expected_days = has_right.astype(jnp.int32) + 2 * (day > 1).astype(jnp.int32)
+    expected_edges = first_chip.astype(jnp.int32)
     for there, db in [(has_north, -REACH), (has_south, REACH)] + [
         (place_exists(dx, dz), dx + REACH * dz) for dx, dz in PLACES
     ]:
@@ -91,11 +93,22 @@
     @pl.when(second_core)
     def _():
         pl.semaphore_wait(barrier, expected_days)
+
+    @pl.when(second_core & ~first_chip)
+    def _():
         tell(days_ready, day - 1)
 
-    @pl.when(first_core)
+    @pl.when(first_core & ~first_chip)
     def _():
         pl.semaphore_wait(days_ready, 1)
+
+    def edges_entered():
+        pl.semaphore_wait(barrier, expected_edges)
+        tell(edges_ready, day + 1)
+
+    @pl.when(first_core & first_chip)
+    def _():
+        edges_entered()
 
     def bulk_row(j):
         at = 16 + j * (STEP * SLOTS)
@@ -117,7 +130,7 @@
             device_id={"blk": blk, "day": day + (1 if side == 0 else -1)}, device_id_type=MESH,
         )
 
-    for side, there in ((0, has_right), (1, has_left)):
+    for side, there in ((0, has_right), (1, day > 1)):
         @pl.when(there)
         def _(side=side):
             for item in range(1, 3 + AHEAD):
@@ -213,16 +226,26 @@
                 total = total + (pltpu.roll(part, shift, 1) if shift else part)
         pack[t * SLOTS : (t + 1) * SLOTS, :] = total
 
-    for side, there in ((0, has_right), (1, has_left)):
+    def send_rest(side):
+        y_copy(side, 0).start()
+
+        def send(j, carry):
+            y_copy(side, j).start()
+            return carry
+
+        lax.fori_loop(3 + AHEAD, 3 + CHUNKS, send, 0)
+
+    for side, there in ((0, has_right), (1, day > 1)):
         @pl.when(there)
         def _(side=side):
-            y_copy(side, 0).start()
-
-            def send(j, carry):
-                y_copy(side, j).start()
-                return carry
-
-            lax.fori_loop(3 + AHEAD, 3 + CHUNKS, send, 0)
+            send_rest(side)
+
+    @pl.when(second_core & first_chip)
+    def _():
+        pl.semaphore_wait(edges_ready, 1)
+        for item in range(1, 3 + AHEAD):
+            y_copy(1, item).start()
+        send_rest(1)
 
     def y_wait(item):
         for side, there in ((0, has_left), (1, has_right)):
@@ -308,12 +331,11 @@
             device_id_type=MESH,
         )
 
-    @pl.when(first_core)
-    def _():
-        pl.semaphore_wait(barrier, expected_edges)
-        tell(edges_ready, day + 1)
-
-    @pl.when(second_core)
+    @pl.when(first_core & ~first_chip)
+    def _():
+        edges_entered()
+
+    @pl.when(second_core & ~first_chip)
     def _():
         pl.semaphore_wait(edges_ready, 1)
 

time: 18.9 us -> 18.5 us (0.979)
  the two profiles are of different devices: /device:TPU:8 before, /device:TPU:1 now
where the time goes in v5:
time: 18.5 us; the launch traced here: 18.3 us
  Pallas kernels  17.5 us (95%)
  local copies, waits for them, and re-layouts  0.88 us (5%)
    pallas_call x1, Pallas kernels, shards(): pl.pallas_call(kernel, out_shape=vmem((SERIES, ROWS, 128), f32), in_specs...  17.5 us
    unnamed x1, local copies, waits for them, and re-layouts  0.88 us

profile of v5, /device:TPU:1, one launch (start us, length us, event | category | flops | bytes accessed | tf_op | source)
XLA Modules:
  0.0 18.3 jit_solution(9494465145056325897)
XLA Ops:
  0.0 17.5 %shard_map.64 = f32[6,256,128]{2,1,0:T(8,128)S(1)} custom-call(f32[6,256,128]{2,1,0:T(8,128)} %bitcast.11, s32[8,8]{1,0:T(8,128)} %nbr_hbm.1, s32[8]{0:T(128)} %act_hbm.1, f32[4]{0:T(128)} %time_hbm.1, f32[2,5]{1,0:T(2,128)} %space_hbm.1, f32[2,2]{1,0:T(2,128)} %factor_hbm.1), custom_call_target="tpu_custom_call" | custom-call | tf_op jit(solution)/shard_map/pallas_call | solution.py:514
  17.5 0.9 %copy.8 = f32[2,3,8,4096]{3,2,1,0:T(8,128)} copy(f32[2,3,8,4096]{3,2,1,0:T(8,128)S(1)} %bitcast.10) | data formatting | bytes 1572864

commit v6 on v5

--- a/solution.py
+++ b/solution.py
@@ -17,7 +17,7 @@
 STEP = 4
 CHUNKS = (TILES - 4) // STEP
 AHEAD = 0
-EARLY = 3
+EARLY = 4
 NONE = -(1 << 20)
 
 EAST, WEST, NORTH, SOUTH, NE, NW, SE, SW = range(8)
@@ -28,8 +28,8 @@
 def kernel(
     x_hbm, nbr_hbm, act_hbm, time_hbm, space_hbm, factor_hbm, done,
     own, left, right, pack, pack_left, pack_right, pack_mixed, packs,
-    mixed, strip_n, strip_s, halo, lhs, weights, across, swapped,
-    take_index, take_mask, edge_mask, live_mask,
+    mixed, strip_n, strip_s, halo, lhs, weights, side_lhs, side_weights, fix, across, swapped,
+    take_index, take_mask, edge_mask, fix_mask, live_mask,
     nbr, act, time_taps, space_taps, factor,
     load_sem, small_sem, y_send, y_recv, z_send, z_recv, p_send, p_recv,
     days_ready, edges_ready,
@@ -165,6 +165,8 @@
     for index, (east, west, dz) in enumerate(((EAST, WEST, 0), (NE, NW, -1), (SE, SW, 1))):
         there = (low & on(named(east), REACH * dz + 1)) | (high & on(named(west), REACH * dz - 1))
         edge_mask[index] = jnp.where(there, 1.0, 0.0).astype(f32)
+    there = (high & on(named(EAST), 1)) | (low & on(named(WEST), -1))
+    fix_mask[...] = jnp.where(there, 1.0, 0.0).astype(f32)
     at_east = on(named(EAST), 1) | on(named(NE), 1 - REACH) | on(named(SE), 1 + REACH)
     at_west = on(named(WEST), -1) | on(named(NW), -1 - REACH) | on(named(SW), -1 + REACH)
     ends = jnp.where((high & at_east) | (low & at_west), 1.0, 0.0).astype(f32)
@@ -273,7 +275,11 @@
     weight_high = weight.astype(bf16)
     weights[0:256, :] = weight_high
     weights[256:512, :] = weight_high
-    weights[512:768, :] = (weight - weight_high.astype(f32)).astype(bf16)
+    weight_low = (weight - weight_high.astype(f32)).astype(bf16)
+    weights[512:768, :] = weight_low
+    side_weights[0:128, :] = weight_high[128:]
+    side_weights[128:256, :] = weight_high[128:]
+    side_weights[256:384, :] = weight_low[128:]
 
     def filtered(v):
         return [
@@ -349,13 +355,65 @@
         def _(side=side):
             z_copy(side).start()
 
+    def take(value, index):
+        return jnp.take_along_axis(value, take_index[index], axis=0) * take_mask[index]
+
+    def own_side(series, at):
+        return take(mixed[series, pl.ds(at, SLOTS), :], 0)
+
+    def split(value):
+        top = value.astype(bf16)
+        return top, (value - top.astype(f32)).astype(bf16)
+
+    def stage(series, centres, side_tiles):
+        span = pl.ds(pl.multiple_of(series * (STEP * SLOTS), 8), STEP * SLOTS)
+        for column, value in ((0, centres), (128, jnp.concatenate(side_tiles, axis=0))):
+            top, rest = split(value)
+            lhs[span, column : column + 128] = top
+            lhs[span, 256 + column : 384 + column] = rest
+            lhs[span, 512 + column : 640 + column] = top
+
+    def filter_across(first_at, second_at):
+        result = jnp.dot(lhs[...], weights[...], preferred_element_type=f32)
+        half = STEP * SLOTS // 2
+        for series in range(SERIES):
+            for at, row in ((first_at, 2 * series), (second_at, 2 * series + 1)):
+                part = result[row * half : (row + 1) * half]
+                across[series, pl.ds(at, half), :] = part[:, :128]
+                swapped[series, pl.ds(at, half), :] = part[:, 128:]
+
+    def across_chunk(j, sides_of):
+        first = bulk_row(j)
+
+        def stage_step(series, inner):
+            side_tiles = [sides_of(series, first + n * SLOTS, n) for n in range(STEP)]
+            stage(series, mixed[series, pl.ds(first, STEP * SLOTS), :], side_tiles)
+            return inner
+
+        lax.fori_loop(0, SERIES, stage_step, 0)
+        filter_across(first + 16, first + 32)
+
+    def rim_stage(series, carry):
+        spots = [tile * SLOTS for tile in (0, 1, TILES - 2, TILES - 1)]
+        centres = [mixed[series, at : at + SLOTS, :] for at in spots]
+        stage(series, jnp.concatenate(centres, axis=0), [own_side(series, at) for at in spots])
+        return carry
+
+    lax.fori_loop(0, SERIES, rim_stage, 0)
+    filter_across(16, ROWS)
+
     def mix_chunk(j, carry):
         y_wait(j + 3)
         for n in range(STEP):
             mix_tile(bulk_row(j) + n * SLOTS)
         return carry
 
-    lax.fori_loop(0, EARLY, mix_chunk, 0)
+    def early_chunk(j, carry):
+        mix_chunk(j, carry)
+        across_chunk(j, lambda series, at, n: own_side(series, at))
+        return carry
+
+    lax.fori_loop(0, EARLY, early_chunk, 0)
 
     for index, (dx, dz) in enumerate(PLACES):
         @pl.when(place_exists(dx, dz))
@@ -378,59 +436,49 @@
                     value = pltpu.roll(both, 128 - shift, 1) if shift else both
                     halo[index, c * DAYS + t, q] = value
 
-    def take(value, index):
-        return jnp.take_along_axis(value, take_index[index], axis=0) * take_mask[index]
-
-    def own_side(series, at, g, q):
-        side = take(mixed[series, pl.ds(at, SLOTS), :], 0)
-        return side + halo[0, series, q, pl.ds(g, 1), :] * edge_mask[0]
-
-    def stage(series, centres, side_tiles):
-        span = pl.ds(pl.multiple_of(series * (STEP * SLOTS), 8), STEP * SLOTS)
-        for column, value in ((0, centres), (128, jnp.concatenate(side_tiles, axis=0))):
-            top = value.astype(bf16)
-            rest = (value - top.astype(f32)).astype(bf16)
-            lhs[span, column : column + 128] = top
-            lhs[span, 256 + column : 384 + column] = rest
-            lhs[span, 512 + column : 640 + column] = top
-
-    def filter_across(at):
-        result = jnp.dot(lhs[...], weights[...], preferred_element_type=f32)
-        for series in range(SERIES):
-            part = result[series * STEP * SLOTS : (series + 1) * STEP * SLOTS]
-            across[series, pl.ds(at, STEP * SLOTS), :] = part[:, :128]
-            swapped[series, pl.ds(at, STEP * SLOTS), :] = part[:, 128:]
-
-    def north_stage(series, carry):
+    def side_stage(series, carry):
+        span = pl.ds(pl.multiple_of(series * (4 * SLOTS), 8), 4 * SLOTS)
+        value = jnp.concatenate([halo[0, series, q] for q in range(4)], axis=0)
+        top, rest = split(value)
+        side_lhs[span, 0:128] = top
+        side_lhs[span, 128:256] = rest
+        side_lhs[span, 256:384] = top
+        return carry
+
+    lax.fori_loop(0, SERIES, side_stage, 0)
+    added = jnp.dot(side_lhs[...], side_weights[...], preferred_element_type=f32)
+    fix[0] = added[:, :128]
+    fix[1] = added[:, 128:]
+
+    def outer_stage(series, carry):
         centres, side_tiles = [], []
-        for tile in range(2):
-            value = strip_n[series, tile * SLOTS : (tile + 1) * SLOTS, :]
-            centres.append(take(value, 1))
-            edge = halo[1, series, 2 + tile, SLOTS - 1 : SLOTS, :] * edge_mask[1]
-            side_tiles.append(take(value, 2) + edge)
-        for tile in range(2):
-            centres.append(mixed[series, tile * SLOTS : (tile + 1) * SLOTS, :])
-            side_tiles.append(own_side(series, tile * SLOTS, 0, tile))
+        for strip, index, edge, tiles, g in (
+            (strip_n, 1, 1, (2, 3), SLOTS - 1), (strip_s, 3, 2, (0, 1), 0)
+        ):
+            for n, q in enumerate(tiles):
+                value = strip[series, n * SLOTS : (n + 1) * SLOTS, :]
+                centres.append(take(value, index))
+                side = halo[edge, series, q, g : g + 1, :] * edge_mask[edge]
+                side_tiles.append(take(value, index + 1) + side)
         stage(series, jnp.concatenate(centres, axis=0), side_tiles)
         return carry
 
-    def south_stage(series, carry):
-        centres, side_tiles = [], []
-        for tile in range(TILES - 2, TILES):
-            centres.append(mixed[series, tile * SLOTS : (tile + 1) * SLOTS, :])
-            side_tiles.append(own_side(series, tile * SLOTS, SLOTS - 1, tile % 4))
-        for tile in range(2):
-            value = strip_s[series, tile * SLOTS : (tile + 1) * SLOTS, :]
-            centres.append(take(value, 3))
-            edge = halo[2, series, tile, 0:1, :] * edge_mask[2]
-            side_tiles.append(take(value, 4) + edge)
-        stage(series, jnp.concatenate(centres, axis=0), side_tiles)
+    lax.fori_loop(0, SERIES, outer_stage, 0)
+    filter_across(0, ROWS + 16)
+
+    def add_fix(series, at, g, q):
+        row = (series * 4 + q) * SLOTS + g
+        span = pl.ds(at + 2 * SLOTS, SLOTS)
+        m = fix_mask[...]
+        across[series, span, :] = across[series, span, :] + fix[0, pl.ds(row, 1), :] * m
+        swapped[series, span, :] = swapped[series, span, :] + fix[1, pl.ds(row, 1), :] * m
+
+    def rim_fix(series, carry):
+        for tile in (0, 1, TILES - 2, TILES - 1):
+            add_fix(series, tile * SLOTS, tile // 4, tile % 4)
         return carry
 
-    lax.fori_loop(0, SERIES, north_stage, 0)
-    filter_across(0)
-    lax.fori_loop(0, SERIES, south_stage, 0)
-    filter_across(ROWS)
+    lax.fori_loop(0, SERIES, rim_fix, 0)
 
     first_half = lane < 64
 
@@ -447,31 +495,35 @@
             )
             done[series, pl.ds(base + SLOTS * n, SLOTS), :] = total * m
 
-    def space_chunk(j, carry):
-        first = bulk_row(j)
-
-        def stage_step(series, inner):
-            side_tiles = [
-                own_side(series, first + n * SLOTS, j + (2 + n) // 4, (2 + n) % 4)
-                for n in range(STEP)
-            ]
-            stage(series, mixed[series, pl.ds(first, STEP * SLOTS), :], side_tiles)
-            return inner
-
+    def late_down(j, carry):
         def down_step(series, inner):
             filter_down(series, j * STEP)
             return inner
 
-        lax.fori_loop(0, SERIES, stage_step, 0)
-        filter_across(first + 2 * SLOTS)
-        lax.fori_loop(0, SERIES, down_step, 0)
-        return carry
-
-    lax.fori_loop(0, EARLY, space_chunk, 0)
+        return lax.fori_loop(0, SERIES, down_step, carry)
+
+    def fixed_down(j, carry):
+        first = bulk_row(j)
+
+        def down_step(series, inner):
+            for n in range(STEP):
+                add_fix(series, first + n * SLOTS, j + (2 + n) // 4, (2 + n) % 4)
+            filter_down(series, j * STEP)
+            return inner
+
+        return lax.fori_loop(0, SERIES, down_step, carry)
+
+    lax.fori_loop(0, EARLY, fixed_down, 0)
 
     def bulk(j, carry):
         mix_chunk(j, carry)
-        return space_chunk(j, carry)
+
+        def sides_of(series, at, n):
+            row = halo[0, series, (2 + n) % 4, pl.ds(j + (2 + n) // 4, 1), :]
+            return own_side(series, at) + row * edge_mask[0]
+
+        across_chunk(j, sides_of)
+        return late_down(j, carry)
 
     lax.fori_loop(EARLY, CHUNKS, bulk, 0)
 
@@ -531,11 +583,15 @@
             vmem((3, SERIES, 4, SLOTS, 128), f32),
             vmem((SERIES * STEP * SLOTS, 768), jnp.bfloat16),
             vmem((768, 256), jnp.bfloat16),
+            vmem((SERIES * 4 * SLOTS, 384), jnp.bfloat16),
+            vmem((384, 256), jnp.bfloat16),
+            vmem((2, SERIES * 4 * SLOTS, 128), f32),
             vmem((SERIES, ROWS + 32, 128), f32),
             vmem((SERIES, ROWS + 32, 128), f32),
             vmem((5, SLOTS, 128), jnp.int32),
             vmem((5, SLOTS, 128), f32),
             vmem((3, SLOTS, 128), f32),
+            vmem((SLOTS, 128), f32),
             vmem((SLOTS, 128), f32),
             vmem((SLOTS, 8), jnp.int32),
             pltpu.SMEM((SLOTS,), jnp.int32),

time: 18.5 us -> 17.4 us (0.941)
  Pallas kernels: 17.5 us -> 16.3 us
    pallas_call x1, Pallas kernels: 17.5 us -> 16.3 us  [shards(): pl.pallas_call(kernel, out_shape=vmem((SERIES, ROWS, 128), f32), in_specs...]
where the time goes in v6:
time: 17.4 us; the launch traced here: 17.2 us
  Pallas kernels  16.3 us (94%)
  local copies, waits for them, and re-layouts  0.88 us (5%)
    pallas_call x1, Pallas kernels, shards(): pl.pallas_call(kernel, out_shape=vmem((SERIES, ROWS, 128), f32), in_specs...  16.3 us
    unnamed x1, local copies, waits for them, and re-layouts  0.88 us

profile of v6, /device:TPU:1, one launch (start us, length us, event | category | flops | bytes accessed | tf_op | source)
XLA Modules:
  0.0 17.2 jit_solution(16669760032630810185)
XLA Ops:
  0.0 16.3 %shard_map.64 = f32[6,256,128]{2,1,0:T(8,128)S(1)} custom-call(f32[6,256,128]{2,1,0:T(8,128)} %bitcast.11, s32[8,8]{1,0:T(8,128)} %nbr_hbm.1, s32[8]{0:T(128)} %act_hbm.1, f32[4]{0:T(128)} %time_hbm.1, f32[2,5]{1,0:T(2,128)} %space_hbm.1, f32[2,2]{1,0:T(2,128)} %factor_hbm.1), custom_call_target="tpu_custom_call" | custom-call | tf_op jit(solution)/shard_map/pallas_call | solution.py:566
  16.4 0.9 %copy.8 = f32[2,3,8,4096]{3,2,1,0:T(8,128)} copy(f32[2,3,8,4096]{3,2,1,0:T(8,128)S(1)} %bitcast.10) | data formatting | bytes 1572864

commit v7 on v6

--- a/solution.py
+++ b/solution.py
@@ -18,6 +18,7 @@
 CHUNKS = (TILES - 4) // STEP
 AHEAD = 0
 EARLY = 4
+EARLY_GROUPS = ((0, 1), (2, 3))
 NONE = -(1 << 20)
 
 EAST, WEST, NORTH, SOUTH, NE, NW, SE, SW = range(8)
@@ -48,6 +49,18 @@
             ok = ok & (row + dz >= 0) & (row + dz < rows)
         return ok
 
+    small = [
+        pltpu.make_async_copy(source, target, small_sem.at[index])
+        for index, (source, target) in enumerate((
+            (nbr_hbm, nbr), (act_hbm, act), (time_hbm, time_taps), (space_hbm, space_taps),
+            (factor_hbm, factor),
+        ))
+    ]
+    load = pltpu.make_async_copy(x_hbm, own, load_sem)
+    load.start()
+    for copy in small:
+        copy.start()
+
     core = day % 2
     chip = day - core
     first_core, second_core = core == 0, core == 1
@@ -77,18 +90,6 @@
     ]:
         hello(there, db, chip)
         expected_edges = expected_edges + 2 * there.astype(jnp.int32)
-
-    small = [
-        pltpu.make_async_copy(source, target, small_sem.at[index])
-        for index, (source, target) in enumerate((
-            (nbr_hbm, nbr), (act_hbm, act), (time_hbm, time_taps), (space_hbm, space_taps),
-            (factor_hbm, factor),
-        ))
-    ]
-    for copy in small:
-        copy.start()
-    load = pltpu.make_async_copy(x_hbm, own, load_sem)
-    load.start()
 
     @pl.when(second_core)
     def _():
@@ -299,8 +300,31 @@
             mixed[t, span, :] = (k00 * f[0][t] + k01 * f[1][t]) * m
             mixed[DAYS + t, span, :] = (k01 * f[0][t] + k11 * f[1][t]) * m
 
-    for item in range(3):
-        y_wait(item)
+    def p_copy(index):
+        dx, dz = PLACES[index]
+        return pltpu.make_async_remote_copy(
+            src_ref=pack_mixed, dst_ref=packs.at[OPPOSITE[index]],
+            send_sem=p_send.at[index], recv_sem=p_recv.at[OPPOSITE[index]],
+            device_id={"blk": blk + dx + REACH * dz, "day": day}, device_id_type=MESH,
+        )
+
+    def p_arrival(index):
+        return pltpu.make_async_remote_copy(
+            src_ref=pack_mixed, dst_ref=packs.at[index],
+            send_sem=p_send.at[index], recv_sem=p_recv.at[index],
+            device_id={"blk": blk, "day": day}, device_id_type=MESH,
+        )
+
+    def z_copy(side):
+        span = pl.ds(ROWS - 16, 16) if side == 0 else pl.ds(0, 16)
+        return pltpu.make_async_remote_copy(
+            src_ref=mixed.at[:, span, :], dst_ref=strip_n if side == 0 else strip_s,
+            send_sem=z_send.at[side], recv_sem=z_recv.at[side],
+            device_id={"blk": blk + (REACH if side == 0 else -REACH), "day": day},
+            device_id_type=MESH,
+        )
+
+    y_wait(0)
     v = [
         ref[t * SLOTS : (t + 1) * SLOTS, :]
         for ref in (pack_left, pack, pack_right) for t in range(DAYS)
@@ -310,32 +334,6 @@
         first_part = k00 * f + k01 * pltpu.roll(f, 96, 1)
         second_part = k11 * f + k01 * pltpu.roll(f, 32, 1)
         pack_mixed[t * SLOTS : (t + 1) * SLOTS, :] = jnp.where(second, second_part, first_part)
-    for tile in (0, 1, TILES - 2, TILES - 1):
-        mix_tile(tile * SLOTS)
-
-    def p_copy(index):
-        dx, dz = PLACES[index]
-        return pltpu.make_async_remote_copy(
-            src_ref=pack_mixed, dst_ref=packs.at[OPPOSITE[index]],
-            send_sem=p_send.at[index], recv_sem=p_recv.at[OPPOSITE[index]],
-            device_id={"blk": blk + dx + REACH * dz, "day": day}, device_id_type=MESH,
-        )
-
-    def p_arrival(index):
-        return pltpu.make_async_remote_copy(
-            src_ref=pack_mixed, dst_ref=packs.at[index],
-            send_sem=p_send.at[index], recv_sem=p_recv.at[index],
-            device_id={"blk": blk, "day": day}, device_id_type=MESH,
-        )
-
-    def z_copy(side):
-        span = pl.ds(ROWS - 16, 16) if side == 0 else pl.ds(0, 16)
-        return pltpu.make_async_remote_copy(
-            src_ref=mixed.at[:, span, :], dst_ref=strip_n if side == 0 else strip_s,
-            send_sem=z_send.at[side], recv_sem=z_recv.at[side],
-            device_id={"blk": blk + (REACH if side == 0 else -REACH), "day": day},
-            device_id_type=MESH,
-        )
 
     @pl.when(first_core & ~first_chip)
     def _():
@@ -350,6 +348,11 @@
         def _(index=index):
             p_copy(index).start()
 
+    for item in (1, 2):
+        y_wait(item)
+    for tile in (0, 1, TILES - 2, TILES - 1):
+        mix_tile(tile * SLOTS)
+
     for side, there in ((0, has_south), (1, has_north)):
         @pl.when(there)
         def _(side=side):
@@ -365,33 +368,42 @@
         top = value.astype(bf16)
         return top, (value - top.astype(f32)).astype(bf16)
 
-    def stage(series, centres, side_tiles):
-        span = pl.ds(pl.multiple_of(series * (STEP * SLOTS), 8), STEP * SLOTS)
+    block_rows = SERIES * STEP * SLOTS
+
+    def stage(series, centres, side_tiles, block=0):
+        at = block * block_rows + series * (STEP * SLOTS)
+        span = pl.ds(pl.multiple_of(at, 8), STEP * SLOTS)
         for column, value in ((0, centres), (128, jnp.concatenate(side_tiles, axis=0))):
             top, rest = split(value)
             lhs[span, column : column + 128] = top
             lhs[span, 256 + column : 384 + column] = rest
-            lhs[span, 512 + column : 640 + column] = top
-
-    def filter_across(first_at, second_at):
-        result = jnp.dot(lhs[...], weights[...], preferred_element_type=f32)
+
+    def filter_across(*blocks):
+        count = len(blocks) * block_rows
+        result = jnp.dot(lhs[0:count, :], weights[0:512, :], preferred_element_type=f32)
+        result = result + jnp.dot(
+            lhs[0:count, 0:256], weights[512:768, :], preferred_element_type=f32
+        )
         half = STEP * SLOTS // 2
-        for series in range(SERIES):
-            for at, row in ((first_at, 2 * series), (second_at, 2 * series + 1)):
-                part = result[row * half : (row + 1) * half]
-                across[series, pl.ds(at, half), :] = part[:, :128]
-                swapped[series, pl.ds(at, half), :] = part[:, 128:]
-
-    def across_chunk(j, sides_of):
+        for block, places in enumerate(blocks):
+            for series in range(SERIES):
+                for n, at in enumerate(places):
+                    row = block * block_rows + (2 * series + n) * half
+                    part = result[row : row + half]
+                    across[series, pl.ds(at, half), :] = part[:, :128]
+                    swapped[series, pl.ds(at, half), :] = part[:, 128:]
+
+    def stage_chunk(j, sides_of, block=0):
         first = bulk_row(j)
 
         def stage_step(series, inner):
             side_tiles = [sides_of(series, first + n * SLOTS, n) for n in range(STEP)]
-            stage(series, mixed[series, pl.ds(first, STEP * SLOTS), :], side_tiles)
+            centres = mixed[series, pl.ds(first, STEP * SLOTS), :]
+            stage(series, centres, side_tiles, block)
             return inner
 
         lax.fori_loop(0, SERIES, stage_step, 0)
-        filter_across(first + 16, first + 32)
+        return first + 16, first + 32
 
     def rim_stage(series, carry):
         spots = [tile * SLOTS for tile in (0, 1, TILES - 2, TILES - 1)]
@@ -400,7 +412,7 @@
         return carry
 
     lax.fori_loop(0, SERIES, rim_stage, 0)
-    filter_across(16, ROWS)
+    blocks = [(16, ROWS)]
 
     def mix_chunk(j, carry):
         y_wait(j + 3)
@@ -408,22 +420,17 @@
             mix_tile(bulk_row(j) + n * SLOTS)
         return carry
 
-    def early_chunk(j, carry):
-        mix_chunk(j, carry)
-        across_chunk(j, lambda series, at, n: own_side(series, at))
-        return carry
-
-    lax.fori_loop(0, EARLY, early_chunk, 0)
+    for group in EARLY_GROUPS:
+        lax.fori_loop(group[0], group[-1] + 1, mix_chunk, 0)
+        for j in group:
+            blocks.append(stage_chunk(j, lambda series, at, n: own_side(series, at), len(blocks)))
+        filter_across(*blocks)
+        blocks = []
 
     for index, (dx, dz) in enumerate(PLACES):
         @pl.when(place_exists(dx, dz))
         def _(index=index):
             p_arrival(index).wait_recv()
-
-    for side, there in ((0, has_north), (1, has_south)):
-        @pl.when(there)
-        def _(side=side):
-            z_copy(side).wait_recv()
 
     west_lanes = (lane & 7) < 4
     for t in range(DAYS):
@@ -449,6 +456,11 @@
     added = jnp.dot(side_lhs[...], side_weights[...], preferred_element_type=f32)
     fix[0] = added[:, :128]
     fix[1] = added[:, 128:]
+
+    for side, there in ((0, has_north), (1, has_south)):
+        @pl.when(there)
+        def _(side=side):
+            z_copy(side).wait_recv()
 
     def outer_stage(series, carry):
         centres, side_tiles = [], []
@@ -464,7 +476,7 @@
         return carry
 
     lax.fori_loop(0, SERIES, outer_stage, 0)
-    filter_across(0, ROWS + 16)
+    filter_across((0, ROWS + 16))
 
     def add_fix(series, at, g, q):
         row = (series * 4 + q) * SLOTS + g
@@ -522,7 +534,7 @@
             row = halo[0, series, (2 + n) % 4, pl.ds(j + (2 + n) // 4, 1), :]
             return own_side(series, at) + row * edge_mask[0]
 
-        across_chunk(j, sides_of)
+        filter_across(stage_chunk(j, sides_of))
         return late_down(j, carry)
 
     lax.fori_loop(EARLY, CHUNKS, bulk, 0)
@@ -581,7 +593,7 @@
             vmem((SERIES, 16, 128), f32),
             vmem((SERIES, 16, 128), f32),
             vmem((3, SERIES, 4, SLOTS, 128), f32),
-            vmem((SERIES * STEP * SLOTS, 768), jnp.bfloat16),
+            vmem((3 * SERIES * STEP * SLOTS, 512), jnp.bfloat16),
             vmem((768, 256), jnp.bfloat16),
             vmem((SERIES * 4 * SLOTS, 384), jnp.bfloat16),
             vmem((384, 256), jnp.bfloat16),

time: 17.4 us -> 17.4 us (level)
  no operation moved by 1% of the time
where the time goes in v7:
time: 17.4 us; the launch traced here: 17.2 us
  Pallas kernels  16.3 us (94%)
  local copies, waits for them, and re-layouts  0.88 us (5%)
    pallas_call x1, Pallas kernels, shards(): pl.pallas_call(kernel, out_shape=vmem((SERIES, ROWS, 128), f32), in_specs...  16.3 us
    unnamed x1, local copies, waits for them, and re-layouts  0.88 us

profile of v7, /device:TPU:1, one launch (start us, length us, event | category | flops | bytes accessed | tf_op | source)
XLA Modules:
  0.0 17.2 jit_solution(2434651839152919519)
XLA Ops:
  0.0 16.3 %shard_map.64 = f32[6,256,128]{2,1,0:T(8,128)S(1)} custom-call(f32[6,256,128]{2,1,0:T(8,128)} %bitcast.11, s32[8,8]{1,0:T(8,128)} %nbr_hbm.1, s32[8]{0:T(128)} %act_hbm.1, f32[4]{0:T(128)} %time_hbm.1, f32[2,5]{1,0:T(2,128)} %space_hbm.1, f32[2,2]{1,0:T(2,128)} %factor_hbm.1), custom_call_target="tpu_custom_call" | custom-call | tf_op jit(solution)/shard_map/pallas_call | solution.py:578
  16.3 0.9 %copy.8 = f32[2,3,8,4096]{3,2,1,0:T(8,128)} copy(f32[2,3,8,4096]{3,2,1,0:T(8,128)S(1)} %bitcast.10) | data formatting | bytes 1572864

commit v8 on v7

--- a/solution.py
+++ b/solution.py
@@ -18,6 +18,7 @@
 CHUNKS = (TILES - 4) // STEP
 AHEAD = 0
 EARLY = 4
+LAST = 8
 EARLY_GROUPS = ((0, 1), (2, 3))
 NONE = -(1 << 20)
 
@@ -27,9 +28,9 @@
 
 
 def kernel(
-    x_hbm, nbr_hbm, act_hbm, time_hbm, space_hbm, factor_hbm, done,
+    x_hbm, nbr_hbm, act_hbm, time_hbm, space_hbm, factor_hbm, done, across, swapped, shared,
     own, left, right, pack, pack_left, pack_right, pack_mixed, packs,
-    mixed, strip_n, strip_s, halo, lhs, weights, side_lhs, side_weights, fix, across, swapped,
+    mixed, strip_n, strip_s, halo, lhs, weights, side_lhs, side_weights, fix,
     take_index, take_mask, edge_mask, fix_mask, live_mask,
     nbr, act, time_taps, space_taps, factor,
     load_sem, small_sem, y_send, y_recv, z_send, z_recv, p_send, p_recv,
@@ -179,6 +180,9 @@
     for s in range(SLOTS):
         live = jnp.where(slot == s, act[s].astype(f32), live)
     live_mask[...] = live
+    shared[0:SLOTS, :] = live
+    for tap in range(5):
+        shared[SLOTS + tap : SLOTS + tap + 1, :] = jnp.full((1, 128), space_taps[1, tap], f32)
 
     @pl.when(jnp.logical_not(has_left))
     def _():
@@ -535,15 +539,14 @@
             return own_side(series, at) + row * edge_mask[0]
 
         filter_across(stage_chunk(j, sides_of))
-        return late_down(j, carry)
+
+        @pl.when(j < CHUNKS - 1)
+        def _():
+            late_down(j, 0)
+
+        return carry
 
     lax.fori_loop(EARLY, CHUNKS, bulk, 0)
-
-    def last_step(series, carry):
-        filter_down(series, TILES - STEP)
-        return carry
-
-    lax.fori_loop(0, SERIES, last_step, 0)
 
     for side, there in ((0, has_right), (1, has_left)):
         @pl.when(there)
@@ -566,6 +569,36 @@
         @pl.when(there)
         def _(side=side):
             z_copy(side).wait_send()
+
+
+def write_out(source, across, swapped, shared, target, rest, sems):
+    first = (TILES - LAST) * SLOTS
+    early = pltpu.make_async_copy(
+        source.at[:, 0:first, :], target.at[:, 0:first, :], sems.at[SERIES]
+    )
+    early.start()
+    m = shared[0:SLOTS, :]
+    d = [shared[SLOTS + tap : SLOTS + tap + 1, :] for tap in range(5)]
+    first_half = lax.broadcasted_iota(jnp.int32, (SLOTS, 128), 1) < 64
+    copies = []
+    for series in range(SERIES):
+        spans = [slice(first + SLOTS * n, first + SLOTS * (n + 1)) for n in range(LAST + 4)]
+        s = [across[series, span, :] for span in spans]
+        b = [swapped[series, span, :] for span in spans]
+        o = [jnp.where(first_half, b[n], b[n + 1]) for n in range(LAST + 3)]
+        for n in range(LAST):
+            total = (
+                d[0] * s[n + 2] + d[1] * (o[n + 2] + o[n + 1]) + d[2] * (s[n + 3] + s[n + 1])
+                + d[3] * (o[n + 3] + o[n]) + d[4] * (s[n + 4] + s[n])
+            )
+            rest[series, SLOTS * n : SLOTS * (n + 1), :] = total * m
+        copy = pltpu.make_async_copy(
+            rest.at[series], target.at[series, first:ROWS, :], sems.at[series]
+        )
+        copy.start()
+        copies.append(copy)
+    for copy in copies + [early]:
+        copy.wait()
 
 
 def shards(input_field, active_mask, neighbours, time_taps, space_taps, coregion_factor):
@@ -575,11 +608,16 @@
     f32 = jnp.float32
     vmem = pltpu.VMEM
     dma = pltpu.SemaphoreType.DMA
-    out = pl.pallas_call(
+    parts = pl.pallas_call(
         kernel,
-        out_shape=vmem((SERIES, ROWS, 128), f32),
+        out_shape=(
+            vmem((SERIES, ROWS, 128), f32),
+            vmem((SERIES, ROWS + 32, 128), f32),
+            vmem((SERIES, ROWS + 32, 128), f32),
+            vmem((2 * SLOTS, 128), f32),
+        ),
         in_specs=[pl.BlockSpec(memory_space=pl.ANY)] * 6,
-        out_specs=pl.BlockSpec(memory_space=vmem),
+        out_specs=(pl.BlockSpec(memory_space=vmem),) * 4,
         scratch_shapes=[
             vmem((SERIES, ROWS, 128), f32),
             vmem((SERIES, ROWS, 128), f32),
@@ -598,8 +636,6 @@
             vmem((SERIES * 4 * SLOTS, 384), jnp.bfloat16),
             vmem((384, 256), jnp.bfloat16),
             vmem((2, SERIES * 4 * SLOTS, 128), f32),
-            vmem((SERIES, ROWS + 32, 128), f32),
-            vmem((SERIES, ROWS + 32, 128), f32),
             vmem((5, SLOTS, 128), jnp.int32),
             vmem((5, SLOTS, 128), f32),
             vmem((3, SLOTS, 128), f32),
@@ -623,6 +659,14 @@
         ],
         compiler_params=pltpu.CompilerParams(collective_id=0, has_side_effects=True),
     )(tiles, neighbours, active_mask, time_taps, space_taps, coregion_factor)
+    out = pl.pallas_call(
+        write_out,
+        out_shape=jax.ShapeDtypeStruct((SERIES, ROWS, 128), f32),
+        in_specs=[pl.BlockSpec(memory_space=vmem)] * 4,
+        out_specs=pl.BlockSpec(memory_space=pl.ANY),
+        scratch_shapes=[vmem((SERIES, LAST * SLOTS, 128), f32), dma((SERIES + 1,))],
+        name="write_out",
+    )(*[pltpu.with_memory_space_constraint(part, vmem) for part in parts])
     out = out.reshape(2, DAYS, TILES, SLOTS, 128).transpose(0, 1, 3, 2, 4)
     return out.reshape(shape)
 

time: 17.4 us -> 17.2 us (0.989)
  local copies, waits for them, and re-layouts: 0.88 us -> 0 us
  Pallas kernels: 16.3 us -> 17.1 us
    unnamed x1 -> x0, local copies, waits for them, and re-layouts: 0.88 us -> none
    pallas_call x1 -> x2, Pallas kernels: 16.3 us -> 17.1 us  [the longest x1 16.2 us: shards(): pl.pallas_call(kernel, out_shape=(vmem((SERIES, ROWS, 128), f32), vmem((S...]
where the time goes in v8:
time: 17.2 us; the launch traced here: 17.1 us
  Pallas kernels  17.1 us (99%)
    pallas_call x1, Pallas kernels, shards(): pl.pallas_call(kernel, out_shape=(vmem((SERIES, ROWS, 128), f32), vmem((S...  16.2 us
    pallas_call x1, Pallas kernels, shards(): pl.pallas_call(write_out, out_shape=jax.ShapeDtypeStruct((SERIES, ROWS, 1...  0.93 us

profile of v8, /device:TPU:1, one launch (start us, length us, event | category | flops | bytes accessed | tf_op | source)
XLA Modules:
  0.0 17.1 jit_solution(17892260298985072433)
XLA Ops:
  0.0 16.2 %shard_map.64 = (f32[6,256,128]{2,1,0:T(8,128)S(1)}, f32[6,288,128]{2,1,0:T(8,128)S(1)}, f32[6,288,128]{2,1,0:T(8,128)S(1)}, f32[16,128]{1,0:T(8,128)S(1)}) custom-call(f32[6,256,128]{2,1,0:T(8,128)} %bitcast.10, s32[8,8]{1,0:T(8,128)} %nbr_hbm.1, s32[8]{0:T(128)} %act_hbm.1, f32[4]{0:T(128)} %time_hbm.1, f32[2,5]{1,0:T(2,128)} %space_hbm.1, f32[2,2]{1,0:T(2,128)} %factor_hbm.1), custom_call_target="tpu_custom_call" | custom-call | tf_op jit(solution)/shard_map/pallas_call | solution.py:611
  16.2 0.9 %write_out.1 = f32[6,256,128]{2,1,0:T(8,128)} custom-call(f32[6,256,128]{2,1,0:T(8,128)S(1)} %get-tuple-element.9.source, f32[6,288,128]{2,1,0:T(8,128)S(1)} %get-tuple-element.10.across, f32[6,288,128]{2,1,0:T(8,128)S(1)} %get-tuple-element.11.swapped, f32[16,128]{1,0:T(8,128)S(1)} %get-tuple-element.12.shared), custom_call_target="tpu_custom_call" | custom-call | tf_op jit(solution)/shard_map/write_out/pallas_call | solution.py:662
